TPU v7x, 512 devices: a whole 4x4x16 slice. The times are simulated.
512 devices in a mesh: gz: 32 (over z_hi, x, y), gy: 16 (over z_lo, core).
Axes of the slice: x: 4, y: 4, z: 16 (z_hi: 2, z_lo: 8; z = z_hi * 8 + z_lo), core: 2. Of those that a mesh axis runs over, the one named last changes fastest.
Arguments:
- velocity: bfloat16 [3, 512, 256, 128], P(None, 'gz', 'gy'), may hold values from -6 to 6
- lag_table: int32 [5, 3], replicated, may hold values from -64 to 64, as said below
- filter_index: int32 [5, 16], replicated, may hold values from 0 to 31
- filter_weights: float32 [3, 32], replicated, may hold values from -4 to 4
Outputs:
- transfer: float32 [512, 256, 128], P('gz', 'gy')
Inputs may be any that keep to these rules, and one draw needn't show every extreme that they name: `lag_table`: column 0 is a base x-offset from 0 to 48, column 1 a y lag from -4 to 4, column 2 a z lag from -64 to 64; one lag has z lag exactly 64 and another exactly -64.
All inputs are finite; a program needn't handle non-finite values.
Results may differ from a plain program's by a relative error of at most 0.0004.
Values may be sent and summed in bfloat16 or wider, within the bound.
No kernel may reach another device: no remote copies, remote signals or barrier semaphores. Data moves between devices by JAX's collectives and lax.ppermute only.
A program may use at most 64 MiB of HBM per device.

v0:
```python
import jax
import jax.numpy as jnp
from jax import lax
from jax.sharding import PartitionSpec as P

NLAG = 5
NOFF = 16
YREACH = 4


def extended_2(block, sides, width):
    for axis, dim in sides:
        count = lax.axis_size(axis)
        forward = [(i, i + 1) for i in range(count - 1)]
        forward.append((count - 1, 0))
        backward = [(target, source) for source, target in forward]
        low = lax.ppermute(
            lax.slice_in_dim(block, block.shape[dim] - width, None, axis=dim), axis, forward
        )
        high = lax.ppermute(lax.slice_in_dim(block, 0, width, axis=dim), axis, backward)
        block = jnp.concatenate([low, block, high], axis=dim)
    return block


def from_behind(x, axis, by):
    peers = lax.axis_size(axis)
    return lax.ppermute(x, axis, [(i, (i + by) % peers) for i in range(peers)])


def cubic_sum(shifted, base_field, start, indices, filter_weights, total):
    length = base_field.shape[3]
    doubled = jnp.concatenate([shifted, shifted], axis=3)
    choices_index = jnp.arange(filter_weights.shape[1], dtype=jnp.int32)
    for offset in range(NOFF):
        moved = lax.dynamic_slice_in_dim(doubled, start + offset, length, axis=3)
        diff = moved.astype(jnp.float32) - base_field
        pick = (choices_index == indices[offset]).astype(jnp.float32)
        gradient = jnp.sum(filter_weights * pick[None, :], axis=1)
        along = gradient[0] * diff[0] + gradient[1] * diff[1] + gradient[2] * diff[2]
        energy = diff[0] * diff[0] + diff[1] * diff[1] + diff[2] * diff[2]
        total = total + along * energy
    return total


def per_device(velocity, lag_table, filter_index, filter_weights):
    planes = velocity.shape[1]
    rows = velocity.shape[2]
    length = velocity.shape[3]
    count = lax.axis_size("gz")
    levels = (count - 1).bit_length()
    zero = jnp.int32(0)
    widened = extended_2(velocity, (("gy", 2),), YREACH)
    following = from_behind(widened, "gz", -1)
    extended = jnp.concatenate([widened, following], axis=1)
    base_field = velocity.astype(jnp.float32)
    blocks = []
    distances = []
    remainders = []
    for lag in range(NLAG):
        lag_y = lag_table[lag, 1]
        lag_z = lag_table[lag, 2]
        whole = jnp.floor_divide(lag_z, planes)
        rest = lag_z - whole * planes
        distances.append(jnp.mod(whole, count))
        remainders.append(rest)
        block = lax.dynamic_slice(
            extended, (zero, zero, YREACH + lag_y, zero), (3, 2 * planes, rows, length)
        )
        block = lax.dynamic_slice(block, (zero, rest, zero, zero), (3, planes, rows, length))
        blocks.append(block)
    stacked = jnp.stack(blocks)
    hop_vector = jnp.stack(distances)
    for level in range(levels):
        moved = from_behind(stacked, "gz", -(1 << level))
        take = jnp.bitwise_and(jnp.right_shift(hop_vector, level), 1) == 1
        stacked = jnp.where(take[:, None, None, None, None], moved, stacked)
    blocks = [stacked[lag] for lag in range(NLAG)]
    total = jnp.zeros((planes, rows, length), jnp.float32)
    for lag in range(NLAG):
        shifted = blocks[lag]
        start = lag_table[lag, 0]
        total = cubic_sum(shifted, base_field, start, filter_index[lag], filter_weights, total)
    return total * (0.25 / (NLAG * NOFF))


def solution(mesh):
    in_specs = (P(None, "gz", "gy", None), P(), P(), P())
    out_specs = P("gz", "gy", None)
    return jax.shard_map(
        per_device, mesh=mesh, in_specs=in_specs, out_specs=out_specs, check_vma=False
    )
```

profile of v0, /device:TPU:38, one launch (start us, length us, event | category | flops | bytes accessed | tf_op | source)
XLA Modules:
  0.0 858.0 jit_solution(1476448895058365789)
XLA Ops:
  1.0 1.9 collective-permute-start
  3.0 3.6 collective-permute-start.1
  6.6 2.1 fusion.84
  8.7 2.1 fusion.85
  10.8 1.5 fusion.86
  12.3 2.1 fusion.82
  14.4 2.1 fusion.83
  16.5 1.9 fusion.87
  66.5 1.2 multiply_reduce_fusion.53
  196.0 5.2 collective-permute-start.2
  203.1 4.7 collective-permute-done.2
  208.5 6.5 collective-permute-start.3
  219.2 16.4 %collective-permute-done.3 = bf16[5,3,16,16,128]{4,3,2,1,0:T(8,128)(2,1)S(1)} collective-permute-done((bf16[5,3,16,16,128]{4,3,2,1,0:T(8,128)(2,1)S(1)}, bf16[5,3,16,16,128]{4,3,2,1,0:T(8,128)(2,1)S(1)}, u32[]{:S(2)}, u32[]{:S(2)}) %collective-permute-start.3) | collective-permute-done | bytes 983072 | tf_op jit(solution)/shard_map/ppermute | solution.py:27
  235.8 4.1 collective-permute-start.4
  245.1 42.4 %collective-permute-done.4 = bf16[5,3,16,16,128]{4,3,2,1,0:T(8,128)(2,1)S(1)} collective-permute-done((bf16[5,3,16,16,128]{4,3,2,1,0:T(8,128)(2,1)S(1)}, bf16[5,3,16,16,128]{4,3,2,1,0:T(8,128)(2,1)S(1)}, u32[]{:S(2)}, u32[]{:S(2)}) %collective-permute-start.4) | collective-permute-done | bytes 983072 | tf_op jit(solution)/shard_map/ppermute | solution.py:27
  287.6 1.9 collective-permute-start.5
  295.5 307.2 %collective-permute-done.5 = bf16[5,3,16,16,128]{4,3,2,1,0:T(8,128)(2,1)S(1)} collective-permute-done((bf16[5,3,16,16,128]{4,3,2,1,0:T(8,128)(2,1)S(1)}, bf16[5,3,16,16,128]{4,3,2,1,0:T(8,128)(2,1)S(1)}, u32[]{:S(2)}, u32[]{:S(2)}) %collective-permute-start.5) | collective-permute-done | bytes 983072 | tf_op jit(solution)/shard_map/ppermute | solution.py:27
  602.9 1.9 collective-permute-start.6
  610.8 40.5 %collective-permute-done.6 = bf16[5,3,16,16,128]{4,3,2,1,0:T(8,128)(2,1)S(1)} collective-permute-done((bf16[5,3,16,16,128]{4,3,2,1,0:T(8,128)(2,1)S(1)}, bf16[5,3,16,16,128]{4,3,2,1,0:T(8,128)(2,1)S(1)}, u32[]{:S(2)}, u32[]{:S(2)}) %collective-permute-start.6) | collective-permute-done | bytes 983072 | tf_op jit(solution)/shard_map/ppermute | solution.py:27
  651.4 4.1 collective-permute-start.7
  661.5 24.2 %collective-permute-done.7 = bf16[5,3,16,16,128]{4,3,2,1,0:T(8,128)(2,1)S(1)} collective-permute-done((bf16[5,3,16,16,128]{4,3,2,1,0:T(8,128)(2,1)S(1)}, bf16[5,3,16,16,128]{4,3,2,1,0:T(8,128)(2,1)S(1)}, u32[]{:S(2)}, u32[]{:S(2)}) %collective-permute-start.7) | collective-permute-done | bytes 983072 | tf_op jit(solution)/shard_map/ppermute | solution.py:27
  686.1 1.1 convert_subtract_fusion.78
  687.2 1.9 add_multiply_fusion.34
  689.1 1.1 convert_subtract_fusion.56
  690.2 2.1 add_multiply_fusion.20
  692.3 1.9 add_multiply_fusion.21
  694.2 1.8 add_multiply_fusion.22
  696.1 1.9 add_multiply_fusion.23
  698.0 1.8 add_multiply_fusion.24
  699.8 1.1 convert_subtract_fusion.79
  700.9 1.9 add_multiply_fusion.29
  702.8 2.1 add_multiply_fusion.30
  704.9 1.8 add_multiply_fusion.31
  706.7 1.8 add_multiply_fusion.32
  708.5 1.9 add_multiply_fusion.33
  710.5 1.9 add_multiply_fusion.35
  712.4 1.8 add_multiply_fusion.36
  714.3 1.9 add_multiply_fusion.37
  716.2 1.8 add_multiply_fusion.38
  718.0 1.8 add_multiply_fusion.39
  720.5 2.0 add_multiply_fusion.25
  722.5 2.0 add_multiply_fusion.26
  724.5 1.9 add_multiply_fusion.27
  726.4 1.9 add_multiply_fusion.28
  728.3 1.9 add_multiply_fusion.40
  731.3 2.0 add_multiply_fusion.19
  737.1 1.3 convert_subtract_fusion.25
  742.9 115.1 %fusion.80 = f32[16,16,128]{2,1,0:T(8,128)} fusion(f32[1,16,16,128]{3,2,1,0:T(8,128)S(1)} %add_multiply_fusion.19, f32[1,16,16,128]{3,2,1,0:T(8,128)S(1)} %add_multiply_fusion.20, f32[1,16,16,128]{3,2,1,0:T(8,128)S(1)} %add_multiply_fusion.21, f32[1,16,16,128]{3,2,1,0:T(8,128)S(1)} %add_multiply_fusion.22, f32[1,16,16,128]{3,2,1,0:T(8,128)S(1)} %add_multiply_fusion.23, ...), kind=kLoop, calls=%fused_computation.338 | loop fusion | flops 23527424 | bytes 25821880 | tf_op jit(solution)/shard_map/mul | solution.py:83
  (157 shorter events, 90.9 us)
Async XLA Ops:
  0.0 195.8 %copy-start = (bf16[3,16,16,128]{3,2,1,0:T(8,128)(2,1)S(1)}, bf16[3,16,16,128]{3,2,1,0:T(8,128)(2,1)}, u32[]{:S(2)}) copy-start(bf16[3,16,16,128]{3,2,1,0:T(8,128)(2,1)} %param.4) | copy-start | bytes 589828
  1.0 194.8 %collective-permute-start = (bf16[3,16,4,128]{3,2,1,0:T(4,128)(2,1)S(1)}, bf16[3,16,4,128]{3,2,1,0:T(4,128)(2,1)S(1)}, u32[]{:S(2)}, u32[]{:S(2)}) collective-permute-start(bf16[3,16,4,128]{3,2,1,0:T(4,128)(2,1)S(1)} %get-tuple-element.170), channel_id=1, source_target_pairs={{0,1},{1,2},{2,3},{3,4},{4,5},{5,6},{6,7},{7,8},{8,9},{9,10},{10,1... | collective-permute-start | bytes 147464 | tf_op jit(solution)/shard_map/ppermute | solution.py:17
  3.0 192.8 %collective-permute-start.1 = (bf16[3,16,4,128]{3,2,1,0:T(4,128)(2,1)S(1)}, bf16[3,16,4,128]{3,2,1,0:T(4,128)(2,1)S(1)}, u32[]{:S(2)}, u32[]{:S(2)}) collective-permute-start(bf16[3,16,4,128]{3,2,1,0:T(4,128)(2,1)S(1)} %get-tuple-element.171), channel_id=1, source_target_pairs={{1,0},{2,1},{3,2},{4,3},{5,4},{6,5},{7,6},{8,7},{9,8},{10,9},{11,1... | collective-permute-start | bytes 147464 | tf_op jit(solution)/shard_map/ppermute | solution.py:20
  196.0 11.9 %collective-permute-start.2 = (bf16[3,16,24,128]{3,2,1,0:T(8,128)(2,1)S(1)}, bf16[3,16,24,128]{3,2,1,0:T(8,128)(2,1)S(1)}, u32[]{:S(2)}, u32[]{:S(2)}) collective-permute-start(bf16[3,16,24,128]{3,2,1,0:T(8,128)(2,1)S(1)} %pad_maximum_fusion.1), channel_id=1, source_target_pairs={{0,496},{16,0},{32,16},{48,32},{64,48},{80,64},{96,80},{112,96},{1... | collective-permute-start | bytes 884744 | tf_op jit(solution)/shard_map/ppermute | solution.py:27
  208.0 10.2 %copy-start.1 = (f32[3,32]{1,0:T(4,128)S(1)}, f32[3,32]{1,0:T(4,128)}, u32[]{:S(2)}) copy-start(f32[3,32]{1,0:T(4,128)} %param.7) | copy-start | bytes 1156
  208.5 27.1 %collective-permute-start.3 = (bf16[5,3,16,16,128]{4,3,2,1,0:T(8,128)(2,1)S(1)}, bf16[5,3,16,16,128]{4,3,2,1,0:T(8,128)(2,1)S(1)}, u32[]{:S(2)}, u32[]{:S(2)}) collective-permute-start(bf16[5,3,16,16,128]{4,3,2,1,0:T(8,128)(2,1)S(1)} %bitcast_dynamic-update-slice_fusion), channel_id=1, source_target_pairs={{0,496},{16,0},{32,16},{48,32},{64,48},{80,64},{96,80},{112,96},{1... | collective-permute-start | bytes 2949128 | tf_op jit(solution)/shard_map/ppermute | solution.py:27
  235.8 51.7 %collective-permute-start.4 = (bf16[5,3,16,16,128]{4,3,2,1,0:T(8,128)(2,1)S(1)}, bf16[5,3,16,16,128]{4,3,2,1,0:T(8,128)(2,1)S(1)}, u32[]{:S(2)}, u32[]{:S(2)}) collective-permute-start(bf16[5,3,16,16,128]{4,3,2,1,0:T(8,128)(2,1)S(1)} %broadcast_select_fusion), channel_id=1, source_target_pairs={{0,480},{16,496},{32,0},{48,16},{64,32},{80,48},{96,64},{112,80},{... | collective-permute-start | bytes 2949128 | tf_op jit(solution)/shard_map/ppermute | solution.py:27
  287.6 315.1 %collective-permute-start.5 = (bf16[5,3,16,16,128]{4,3,2,1,0:T(8,128)(2,1)S(1)}, bf16[5,3,16,16,128]{4,3,2,1,0:T(8,128)(2,1)S(1)}, u32[]{:S(2)}, u32[]{:S(2)}) collective-permute-start(bf16[5,3,16,16,128]{4,3,2,1,0:T(8,128)(2,1)S(1)} %broadcast_select_fusion.1), channel_id=1, source_target_pairs={{0,448},{16,464},{32,480},{48,496},{64,0},{80,16},{96,32},{112,48}... | collective-permute-start | bytes 2949128 | tf_op jit(solution)/shard_map/ppermute | solution.py:27
  602.9 48.4 %collective-permute-start.6 = (bf16[5,3,16,16,128]{4,3,2,1,0:T(8,128)(2,1)S(1)}, bf16[5,3,16,16,128]{4,3,2,1,0:T(8,128)(2,1)S(1)}, u32[]{:S(2)}, u32[]{:S(2)}) collective-permute-start(bf16[5,3,16,16,128]{4,3,2,1,0:T(8,128)(2,1)S(1)} %broadcast_select_fusion.2), channel_id=1, source_target_pairs={{0,384},{16,400},{32,416},{48,432},{64,448},{80,464},{96,480},{112... | collective-permute-start | bytes 2949128 | tf_op jit(solution)/shard_map/ppermute | solution.py:27
  651.4 34.3 %collective-permute-start.7 = (bf16[5,3,16,16,128]{4,3,2,1,0:T(8,128)(2,1)S(1)}, bf16[5,3,16,16,128]{4,3,2,1,0:T(8,128)(2,1)S(1)}, u32[]{:S(2)}, u32[]{:S(2)}) collective-permute-start(bf16[5,3,16,16,128]{4,3,2,1,0:T(8,128)(2,1)S(1)} %broadcast_select_fusion.3), channel_id=1, source_target_pairs={{0,256},{16,272},{32,288},{48,304},{64,320},{80,336},{96,352},{112... | collective-permute-start | bytes 2949128 | tf_op jit(solution)/shard_map/ppermute | solution.py:27
where the time goes:
time: 864 us; the launch traced here: 858 us
  waiting for transfers between devices  435 us (50%)
  other arithmetic  225 us (26%)
  between operations  128 us (15%)
  local copies, waits for them, and re-layouts  40.1 us (5%)
  starting transfers between devices  29.3 us (3%)
    ppermute x6, waiting for transfers between devices, from_behind(): return lax.ppermute(x, axis, [(i, (i + by) % peers) for i in range(peers)])  435 us
    mul x1, other arithmetic, per_device(): return total * (0.25 / (NLAG * NOFF))  115 us
    convert_element_type x80, other arithmetic, cubic_sum(): pick = (choices_index == indices[offset]).astype(jnp.float32)  49.9 us
    mul x22, other arithmetic, cubic_sum(): total = total + along * energy  41.8 us
    slice x40, local copies, waits for them, and re-layouts, cubic_sum(): gradient[0] * diff[0] + gradient[1] * diff[1] + gradient[2] * diff[2]  26.5 us
    ppermute x6, starting transfers between devices, from_behind(): return lax.ppermute(x, axis, [(i, (i + by) % peers) for i in range(peers)])  23.7 us
  transfers between devices with their start and end apart: 8, of which 6 were waited for; matrix products, arithmetic and copies ran while one was open for 11% of the time, Pallas kernels for 0%

commit v1 on v0

v1 whole, which is shorter than its diff:
```python
import jax
import jax.numpy as jnp
from jax import lax
from jax.experimental import pallas as pl
from jax.experimental.pallas import tpu as pltpu
from jax.sharding import PartitionSpec as P

NLAG = 5
NOFF = 16
YREACH = 4
PLANES = 16
ROWS = 16
LANES = 128
AXES = ("gz", "gy")


def places():
    return [(h, x, y, g) for h in range(2) for x in range(4) for y in range(4) for g in range(16)]


def number(h, x, y, g):
    return ((h * 4 + x) * 4 + y) * 16 + g


def pairs(to):
    return [(number(*p), number(*to(*p))) for p in places()]


SWAP_A = pairs(lambda h, x, y, g: (h ^ (x % 3 == 0), 3 - x, y, g))
SWAP_B = pairs(lambda h, x, y, g: (h, x ^ 1, y, g))
SWAP_Y = [pairs(lambda h, x, y, g, k=k: (h, x, y ^ k, g)) for k in (1, 2, 3)]
SWAP_E = pairs(lambda h, x, y, g: (h, x, y, g ^ 1))
SWAP_O = pairs(lambda h, x, y, g: (h, x, y, (g + 1) % 16 if g % 2 else (g - 1) % 16))


def send(x, perm):
    return lax.ppermute(x, AXES, perm)


def sums_kernel(
    lag_ref, index_ref, weight_ref, u_ref, a_ref, b_ref, e_ref, o_ref, r1_ref, r2_ref, r3_ref,
    out_ref, field, base, gains,
):
    gz = lax.axis_index("gz")
    y = gz & 3
    odd_x = (gz >> 2) & 1
    odd_g = lax.axis_index("gy") & 1

    for block, ref in enumerate((u_ref, a_ref, b_ref)):
        for c in range(3):
            field[block, c, :, YREACH:YREACH + ROWS, :] = ref[c].astype(jnp.float32)
    for slot, ref in enumerate((u_ref, r1_ref, r2_ref, r3_ref)):
        base[slot] = ref[...].astype(jnp.float32)

    @pl.when(odd_g == 0)
    def _():
        field[:, :, :, 0:YREACH, :] = o_ref[...].astype(jnp.float32)
        field[:, :, :, YREACH + ROWS:, :] = e_ref[...].astype(jnp.float32)

    @pl.when(odd_g == 1)
    def _():
        field[:, :, :, 0:YREACH, :] = e_ref[...].astype(jnp.float32)
        field[:, :, :, YREACH + ROWS:, :] = o_ref[...].astype(jnp.float32)

    out_ref[...] = jnp.zeros_like(out_ref)

    def fill(n, carry):
        lag = n // NOFF
        k = n - lag * NOFF
        row = index_ref[lag, k]
        for c in range(3):
            gains[n, c] = jnp.full((8, LANES), weight_ref[c, row], jnp.float32)
        return carry

    lax.fori_loop(0, NLAG * NOFF, fill, 0)

    def step(n, carry):
        lag = n // PLANES
        plane = n - lag * PLANES
        start = lag_ref[lag, 0]
        lag_y = lag_ref[lag, 1]
        lag_z = lag_ref[lag, 2]
        whole = lag_z >> 4
        rest = lag_z & 15
        hops = whole + jnp.where(plane < rest, 1, 0)
        target = (y - hops) & 3
        column = (target + hops - y) >> 2
        block = jnp.where(column == 0, 0, jnp.where((column > 0) == (odd_x == 0), 2, 1))
        slot = y ^ target
        at = (plane - rest) & 15
        first = YREACH + lag_y
        moved = [
            [field[block, c, plane, pl.ds(first + 8 * half, 8), :] for c in range(3)]
            for half in range(2)
        ]
        here = [
            [base[slot, c, at, 8 * half:8 * half + 8, :] for c in range(3)] for half in range(2)
        ]
        sums = [out_ref[slot, at, 8 * half:8 * half + 8, :] for half in range(2)]
        for k in range(NOFF):
            shift = (2 * LANES - start - k) & (LANES - 1)
            g0, g1, g2 = (gains[lag * NOFF + k, c] for c in range(3))
            for half in range(2):
                d0, d1, d2 = (
                    pltpu.roll(moved[half][c], shift, 1) - here[half][c] for c in range(3)
                )
                along = g0 * d0 + g1 * d1 + g2 * d2
                energy = d0 * d0 + d1 * d1 + d2 * d2
                sums[half] = sums[half] + along * energy
        for half in range(2):
            out_ref[slot, at, 8 * half:8 * half + 8, :] = sums[half]
        return carry

    lax.fori_loop(0, NLAG * PLANES, step, 0)


def partial_sums(lag_table, filter_index, filter_weights, *fields):
    smem = pl.BlockSpec(memory_space=pltpu.SMEM)
    vmem = pl.BlockSpec(memory_space=pltpu.VMEM)
    return pl.pallas_call(
        sums_kernel,
        out_shape=jax.ShapeDtypeStruct((4, PLANES, ROWS, LANES), jnp.float32),
        in_specs=[smem] * 3 + [vmem] * len(fields),
        out_specs=vmem,
        scratch_shapes=[
            pltpu.VMEM((3, 3, PLANES, ROWS + 2 * YREACH, LANES), jnp.float32),
            pltpu.VMEM((4, 3, PLANES, ROWS, LANES), jnp.float32),
            pltpu.VMEM((NLAG * NOFF, 3, 8, LANES), jnp.float32),
        ],
        compiler_params=pltpu.CompilerParams(vmem_limit_bytes=16 << 20),
        name="sums",
    )(lag_table, filter_index, filter_weights, *fields)


def per_device(velocity, lag_table, filter_index, filter_weights):
    odd_g = lax.axis_index("gy") & 1
    a = send(velocity, SWAP_A)
    b = send(velocity, SWAP_B)
    r1, r2, r3 = (send(velocity, perm) for perm in SWAP_Y)
    blocks = jnp.stack([velocity, a, b])
    low = blocks[:, :, :, :YREACH]
    high = blocks[:, :, :, ROWS - YREACH:]
    e = send(jnp.where(odd_g == 0, high, low), SWAP_E)
    o = send(jnp.where(odd_g == 0, low, high), SWAP_O)
    sums = partial_sums(lag_table, filter_index, filter_weights, velocity, a, b, e, o, r1, r2, r3)
    p1, p2, p3 = (send(sums[k + 1], perm) for k, perm in enumerate(SWAP_Y))
    return (sums[0] + p1 + p2 + p3) * (0.25 / (NLAG * NOFF))


def solution(mesh):
    in_specs = (P(None, "gz", "gy", None), P(), P(), P())
    out_specs = P("gz", "gy", None)
    return jax.shard_map(
        per_device, mesh=mesh, in_specs=in_specs, out_specs=out_specs, check_vma=False
    )
```

time: 864 us -> 86.9 us (0.10)
  the two profiles are of different devices: /device:TPU:38 before, /device:TPU:8 now
where the time goes in v1:
time: 86.9 us; the launch traced here: 86.5 us
  starting transfers between devices  49.2 us (57%)
  Pallas kernels  18 us (21%)
  waiting for transfers between devices  17.2 us (20%)
  other arithmetic  1.82 us (2%)
    ppermute x10, starting transfers between devices, send(): return lax.ppermute(x, AXES, perm)  49.2 us
    pallas_call x1, Pallas kernels, partial_sums(): pl.pallas_call(sums_kernel, out_shape=jax.ShapeDtypeStruct((4, PLANES, RO...  18 us
    ppermute x10, waiting for transfers between devices, send(): return lax.ppermute(x, AXES, perm)  17.2 us
  transfers between devices with their start and end apart: 10, of which 3 were waited for; matrix products, arithmetic and copies ran while one was open for 1% of the time, Pallas kernels for 0%

profile of v1, /device:TPU:8, one launch (start us, length us, event | category | flops | bytes accessed | tf_op | source)
XLA Modules:
  0.0 86.5 jit_solution(200081733938214741)
XLA Ops:
  0.0 3.4 %collective-permute-start.1 = (bf16[3,16,16,128]{3,2,1,0:T(8,128)(2,1)}, bf16[3,16,16,128]{3,2,1,0:T(8,128)(2,1)S(1)}, u32[]{:S(2)}, u32[]{:S(2)}) collective-permute-start(bf16[3,16,16,128]{3,2,1,0:T(8,128)(2,1)} %u_ref.1), channel_id=1, source_target_pairs={{0,64},{1,65},{2,66},{3,67},{4,68},{5,69},{6,70},{7,71},{8,72},{9,... | collective-permute-start | bytes 589832 | tf_op jit(solution)/shard_map/ppermute | solution.py:37
  3.4 17.3 %collective-permute-start = (bf16[3,16,16,128]{3,2,1,0:T(8,128)(2,1)}, bf16[3,16,16,128]{3,2,1,0:T(8,128)(2,1)S(1)}, u32[]{:S(2)}, u32[]{:S(2)}) collective-permute-start(bf16[3,16,16,128]{3,2,1,0:T(8,128)(2,1)} %u_ref.1), channel_id=1, source_target_pairs={{0,448},{1,449},{2,450},{3,451},{4,452},{5,453},{6,454},{7,455},{8... | collective-permute-start | bytes 589832 | tf_op jit(solution)/shard_map/ppermute | solution.py:37
  20.7 4.2 %collective-permute-start.5 = (bf16[3,16,16,128]{3,2,1,0:T(8,128)(2,1)}, bf16[3,16,16,128]{3,2,1,0:T(8,128)(2,1)S(1)}, u32[]{:S(2)}, u32[]{:S(2)}) collective-permute-start(bf16[3,16,16,128]{3,2,1,0:T(8,128)(2,1)} %u_ref.1), channel_id=1, source_target_pairs={{0,32},{1,33},{2,34},{3,35},{4,36},{5,37},{6,38},{7,39},{8,40},{9,... | collective-permute-start | bytes 589832 | tf_op jit(solution)/shard_map/ppermute | solution.py:37
  24.9 3.3 %collective-permute-start.4 = (bf16[3,16,16,128]{3,2,1,0:T(8,128)(2,1)}, bf16[3,16,16,128]{3,2,1,0:T(8,128)(2,1)S(1)}, u32[]{:S(2)}, u32[]{:S(2)}) collective-permute-start(bf16[3,16,16,128]{3,2,1,0:T(8,128)(2,1)} %u_ref.1), channel_id=1, source_target_pairs={{0,16},{1,17},{2,18},{3,19},{4,20},{5,21},{6,22},{7,23},{8,24},{9,... | collective-permute-start | bytes 589832 | tf_op jit(solution)/shard_map/ppermute | solution.py:37
  28.1 2.4 %collective-permute-start.6 = (bf16[3,16,16,128]{3,2,1,0:T(8,128)(2,1)}, bf16[3,16,16,128]{3,2,1,0:T(8,128)(2,1)S(1)}, u32[]{:S(2)}, u32[]{:S(2)}) collective-permute-start(bf16[3,16,16,128]{3,2,1,0:T(8,128)(2,1)} %u_ref.1), channel_id=1, source_target_pairs={{0,48},{1,49},{2,50},{3,51},{4,52},{5,53},{6,54},{7,55},{8,56},{9,... | collective-permute-start | bytes 589832 | tf_op jit(solution)/shard_map/ppermute | solution.py:37
  30.5 0.0 collective-permute-done.1.b_ref
  30.5 5.8 %collective-permute-done.a_ref = bf16[3,16,16,128]{3,2,1,0:T(8,128)(2,1)S(1)} collective-permute-done((bf16[3,16,16,128]{3,2,1,0:T(8,128)(2,1)}, bf16[3,16,16,128]{3,2,1,0:T(8,128)(2,1)S(1)}, u32[]{:S(2)}, u32[]{:S(2)}) %collective-permute-start) | collective-permute-done | bytes 196640 | tf_op jit(solution)/shard_map/ppermute | solution.py:37
  36.3 1.1 %broadcast_select_fusion = (bf16[3,3,16,4,128]{4,3,2,1,0:T(4,128)(2,1)S(1)}, bf16[3,3,16,4,128]{4,3,2,1,0:T(4,128)(2,1)S(1)}, bf16[3,3,16,4,128]{4,3,2,1,0:T(4,128)(2,1)S(1)}) fusion(pred[]{:T(512)S(6)} %eq.4, bf16[1,3,16,16,128]{4,3,2,1,0:T(8,128)(2,1)S(1)} %bitcast.23, bf16[1,3,16,16,128]{4,3,2,1,0:T(8,128)(2,1)S(1)} %bitcast.24, ...), kind=kLoop, calls=%fused_computation.3 | loop fusion | flops 958464 | bytes 1032193 | tf_op jit(solution)/shard_map/jit(_where)/select_n | solution.py:144
  37.4 0.0 copy-start
  37.5 0.0 copy-start.3
  37.5 0.0 copy-start.1
  37.5 2.1 %collective-permute-start.2 = (bf16[3,3,16,4,128]{4,3,2,1,0:T(4,128)(2,1)S(1)}, bf16[3,3,16,4,128]{4,3,2,1,0:T(4,128)(2,1)S(1)}, u32[]{:S(2)}, u32[]{:S(2)}) collective-permute-start(bf16[3,3,16,4,128]{4,3,2,1,0:T(4,128)(2,1)S(1)} %bitcast.27), channel_id=1, source_target_pairs={{0,1},{1,0},{2,3},{3,2},{4,5},{5,4},{6,7},{7,6},{8,9},{9,8},{10,11... | collective-permute-start | bytes 442376 | tf_op jit(solution)/shard_map/ppermute | solution.py:37
  39.6 0.0 copy-start.2
  39.6 6.9 %collective-permute-start.3 = (bf16[3,3,16,4,128]{4,3,2,1,0:T(4,128)(2,1)S(1)}, bf16[3,3,16,4,128]{4,3,2,1,0:T(4,128)(2,1)S(1)}, u32[]{:S(2)}, u32[]{:S(2)}) collective-permute-start(bf16[3,3,16,4,128]{4,3,2,1,0:T(4,128)(2,1)S(1)} %get-tuple-element.5), channel_id=1, source_target_pairs={{0,15},{1,2},{2,1},{3,4},{4,3},{5,6},{6,5},{7,8},{8,7},{9,10},{10,... | collective-permute-start | bytes 442376 | tf_op jit(solution)/shard_map/ppermute | solution.py:37
  46.5 0.0 copy-done.3
  46.5 0.1 copy.5.lag_ref
  46.6 0.0 collective-permute-done.5.r2_ref
  46.6 0.0 collective-permute-done.4.r1_ref
  46.6 0.0 collective-permute-done.6.r3_ref
  46.6 0.0 collective-permute-done.2.e_ref
  46.6 6.2 %collective-permute-done.3.o_ref = bf16[3,3,16,4,128]{4,3,2,1,0:T(4,128)(2,1)S(1)} collective-permute-done((bf16[3,3,16,4,128]{4,3,2,1,0:T(4,128)(2,1)S(1)}, bf16[3,3,16,4,128]{4,3,2,1,0:T(4,128)(2,1)S(1)}, u32[]{:S(2)}, u32[]{:S(2)}) %collective-permute-start.3) | collective-permute-done | bytes 147488 | tf_op jit(solution)/shard_map/ppermute | solution.py:37
  52.8 0.0 copy-done
  52.8 0.0 copy-done.1
  52.8 0.0 copy-done.2
  52.8 18.0 %sums.1 = f32[4,16,16,128]{3,2,1,0:T(8,128)S(1)} custom-call(s32[5,3]{1,0:T(8,128)S(1)} %copy.5.lag_ref, s32[5,16]{1,0:T(8,128)S(1)} %copy-done.1, f32[3,32]{1,0:T(4,128)S(1)} %copy-done.2, bf16[3,16,16,128]{3,2,1,0:T(8,128)(2,1)S(1)} %copy-done, bf16[3,16,16,128]{3,2,1,0:T(8,128)(2,1)S(1)} %collective-permute-done.a_ref, ...), custom_call_target="tpu_custom_call" | custom-call | tf_op jit(solution)/shard_map/sums/pallas_call | solution.py:120
  70.8 2.4 %collective-permute-start.7 = (f32[16,16,128]{2,1,0:T(8,128)S(1)}, f32[16,16,128]{2,1,0:T(8,128)S(1)}, u32[]{:S(2)}, u32[]{:S(2)}) collective-permute-start(f32[16,16,128]{2,1,0:T(8,128)S(1)} %get-tuple-element.8), channel_id=1, source_target_pairs={{0,16},{1,17},{2,18},{3,19},{4,20},{5,21},{6,22},{7,23},{8,24},{9,... | collective-permute-start | bytes 393224 | tf_op jit(solution)/shard_map/ppermute | solution.py:37
  73.1 4.3 %collective-permute-start.9 = (f32[16,16,128]{2,1,0:T(8,128)S(1)}, f32[16,16,128]{2,1,0:T(8,128)S(1)}, u32[]{:S(2)}, u32[]{:S(2)}) collective-permute-start(f32[16,16,128]{2,1,0:T(8,128)S(1)} %get-tuple-element.9), channel_id=1, source_target_pairs={{0,48},{1,49},{2,50},{3,51},{4,52},{5,53},{6,54},{7,55},{8,56},{9,... | collective-permute-start | bytes 393224 | tf_op jit(solution)/shard_map/ppermute | solution.py:37
  77.5 3.1 %collective-permute-start.8 = (f32[16,16,128]{2,1,0:T(8,128)S(1)}, f32[16,16,128]{2,1,0:T(8,128)S(1)}, u32[]{:S(2)}, u32[]{:S(2)}) collective-permute-start(f32[16,16,128]{2,1,0:T(8,128)S(1)} %get-tuple-element.10), channel_id=1, source_target_pairs={{0,32},{1,33},{2,34},{3,35},{4,36},{5,37},{6,38},{7,39},{8,40},{9,... | collective-permute-start | bytes 393224 | tf_op jit(solution)/shard_map/ppermute | solution.py:37
  80.6 0.0 collective-permute-done.7
  80.6 0.0 collective-permute-done.9
  80.6 5.2 %collective-permute-done.8 = f32[16,16,128]{2,1,0:T(8,128)S(1)} collective-permute-done((f32[16,16,128]{2,1,0:T(8,128)S(1)}, f32[16,16,128]{2,1,0:T(8,128)S(1)}, u32[]{:S(2)}, u32[]{:S(2)}) %collective-permute-start.8) | collective-permute-done | bytes 131104 | tf_op jit(solution)/shard_map/ppermute | solution.py:37
  85.8 0.7 fusion.3
  (2 shorter events, 0.0 us)
Async XLA Ops:
  0.0 30.5 %collective-permute-start.1 = (bf16[3,16,16,128]{3,2,1,0:T(8,128)(2,1)}, bf16[3,16,16,128]{3,2,1,0:T(8,128)(2,1)S(1)}, u32[]{:S(2)}, u32[]{:S(2)}) collective-permute-start(bf16[3,16,16,128]{3,2,1,0:T(8,128)(2,1)} %u_ref.1), channel_id=1, source_target_pairs={{0,64},{1,65},{2,66},{3,67},{4,68},{5,69},{6,70},{7,71},{8,72},{9,... | collective-permute-start | bytes 589832 | tf_op jit(solution)/shard_map/ppermute | solution.py:37
  3.4 32.9 %collective-permute-start = (bf16[3,16,16,128]{3,2,1,0:T(8,128)(2,1)}, bf16[3,16,16,128]{3,2,1,0:T(8,128)(2,1)S(1)}, u32[]{:S(2)}, u32[]{:S(2)}) collective-permute-start(bf16[3,16,16,128]{3,2,1,0:T(8,128)(2,1)} %u_ref.1), channel_id=1, source_target_pairs={{0,448},{1,449},{2,450},{3,451},{4,452},{5,453},{6,454},{7,455},{8... | collective-permute-start | bytes 589832 | tf_op jit(solution)/shard_map/ppermute | solution.py:37
  20.7 25.9 %collective-permute-start.5 = (bf16[3,16,16,128]{3,2,1,0:T(8,128)(2,1)}, bf16[3,16,16,128]{3,2,1,0:T(8,128)(2,1)S(1)}, u32[]{:S(2)}, u32[]{:S(2)}) collective-permute-start(bf16[3,16,16,128]{3,2,1,0:T(8,128)(2,1)} %u_ref.1), channel_id=1, source_target_pairs={{0,32},{1,33},{2,34},{3,35},{4,36},{5,37},{6,38},{7,39},{8,40},{9,... | collective-permute-start | bytes 589832 | tf_op jit(solution)/shard_map/ppermute | solution.py:37
  24.9 21.7 %collective-permute-start.4 = (bf16[3,16,16,128]{3,2,1,0:T(8,128)(2,1)}, bf16[3,16,16,128]{3,2,1,0:T(8,128)(2,1)S(1)}, u32[]{:S(2)}, u32[]{:S(2)}) collective-permute-start(bf16[3,16,16,128]{3,2,1,0:T(8,128)(2,1)} %u_ref.1), channel_id=1, source_target_pairs={{0,16},{1,17},{2,18},{3,19},{4,20},{5,21},{6,22},{7,23},{8,24},{9,... | collective-permute-start | bytes 589832 | tf_op jit(solution)/shard_map/ppermute | solution.py:37
  28.1 18.4 %collective-permute-start.6 = (bf16[3,16,16,128]{3,2,1,0:T(8,128)(2,1)}, bf16[3,16,16,128]{3,2,1,0:T(8,128)(2,1)S(1)}, u32[]{:S(2)}, u32[]{:S(2)}) collective-permute-start(bf16[3,16,16,128]{3,2,1,0:T(8,128)(2,1)} %u_ref.1), channel_id=1, source_target_pairs={{0,48},{1,49},{2,50},{3,51},{4,52},{5,53},{6,54},{7,55},{8,56},{9,... | collective-permute-start | bytes 589832 | tf_op jit(solution)/shard_map/ppermute | solution.py:37
  37.4 15.3 %copy-start = (bf16[3,16,16,128]{3,2,1,0:T(8,128)(2,1)S(1)}, bf16[3,16,16,128]{3,2,1,0:T(8,128)(2,1)}, u32[]{:S(2)}) copy-start(bf16[3,16,16,128]{3,2,1,0:T(8,128)(2,1)} %u_ref.1) | copy-start | bytes 589828
  37.5 9.0 %copy-start.3 = (s32[5,3]{0,1:T(4,128)S(1)}, s32[5,3]{0,1:T(4,128)}, u32[]{:S(2)}) copy-start(s32[5,3]{0,1:T(4,128)} %param.5) | copy-start | bytes 184
  37.5 15.3 %copy-start.1 = (s32[5,16]{1,0:T(8,128)S(1)}, s32[5,16]{1,0:T(8,128)}, u32[]{:S(2)}) copy-start(s32[5,16]{1,0:T(8,128)} %index_ref.1) | copy-start | bytes 964
  37.5 9.1 %collective-permute-start.2 = (bf16[3,3,16,4,128]{4,3,2,1,0:T(4,128)(2,1)S(1)}, bf16[3,3,16,4,128]{4,3,2,1,0:T(4,128)(2,1)S(1)}, u32[]{:S(2)}, u32[]{:S(2)}) collective-permute-start(bf16[3,3,16,4,128]{4,3,2,1,0:T(4,128)(2,1)S(1)} %bitcast.27), channel_id=1, source_target_pairs={{0,1},{1,0},{2,3},{3,2},{4,5},{5,4},{6,7},{7,6},{8,9},{9,8},{10,11... | collective-permute-start | bytes 442376 | tf_op jit(solution)/shard_map/ppermute | solution.py:37
  39.6 13.2 %copy-start.2 = (f32[3,32]{1,0:T(4,128)S(1)}, f32[3,32]{1,0:T(4,128)}, u32[]{:S(2)}) copy-start(f32[3,32]{1,0:T(4,128)} %weight_ref.1) | copy-start | bytes 1156
  39.6 13.2 %collective-permute-start.3 = (bf16[3,3,16,4,128]{4,3,2,1,0:T(4,128)(2,1)S(1)}, bf16[3,3,16,4,128]{4,3,2,1,0:T(4,128)(2,1)S(1)}, u32[]{:S(2)}, u32[]{:S(2)}) collective-permute-start(bf16[3,3,16,4,128]{4,3,2,1,0:T(4,128)(2,1)S(1)} %get-tuple-element.5), channel_id=1, source_target_pairs={{0,15},{1,2},{2,1},{3,4},{4,3},{5,6},{6,5},{7,8},{8,7},{9,10},{10,... | collective-permute-start | bytes 442376 | tf_op jit(solution)/shard_map/ppermute | solution.py:37
  70.8 9.8 %collective-permute-start.7 = (f32[16,16,128]{2,1,0:T(8,128)S(1)}, f32[16,16,128]{2,1,0:T(8,128)S(1)}, u32[]{:S(2)}, u32[]{:S(2)}) collective-permute-start(f32[16,16,128]{2,1,0:T(8,128)S(1)} %get-tuple-element.8), channel_id=1, source_target_pairs={{0,16},{1,17},{2,18},{3,19},{4,20},{5,21},{6,22},{7,23},{8,24},{9,... | collective-permute-start | bytes 393224 | tf_op jit(solution)/shard_map/ppermute | solution.py:37
  73.1 7.5 %collective-permute-start.9 = (f32[16,16,128]{2,1,0:T(8,128)S(1)}, f32[16,16,128]{2,1,0:T(8,128)S(1)}, u32[]{:S(2)}, u32[]{:S(2)}) collective-permute-start(f32[16,16,128]{2,1,0:T(8,128)S(1)} %get-tuple-element.9), channel_id=1, source_target_pairs={{0,48},{1,49},{2,50},{3,51},{4,52},{5,53},{6,54},{7,55},{8,56},{9,... | collective-permute-start | bytes 393224 | tf_op jit(solution)/shard_map/ppermute | solution.py:37
  77.5 8.4 %collective-permute-start.8 = (f32[16,16,128]{2,1,0:T(8,128)S(1)}, f32[16,16,128]{2,1,0:T(8,128)S(1)}, u32[]{:S(2)}, u32[]{:S(2)}) collective-permute-start(f32[16,16,128]{2,1,0:T(8,128)S(1)} %get-tuple-element.10), channel_id=1, source_target_pairs={{0,32},{1,33},{2,34},{3,35},{4,36},{5,37},{6,38},{7,39},{8,40},{9,... | collective-permute-start | bytes 393224 | tf_op jit(solution)/shard_map/ppermute | solution.py:37

commit v2 on v1

v2 whole, which is shorter than its diff:
```python
import jax
import jax.numpy as jnp
from jax import lax
from jax.experimental import pallas as pl
from jax.experimental.pallas import tpu as pltpu
from jax.sharding import Mesh
from jax.sharding import PartitionSpec as P


NLAG = 5
NOFF = 16
YREACH = 4
PLANES = 16
ROWS = 16
LANES = 128
AXES = ("zh", "x", "y", "zl", "c")
SIZES = (2, 4, 4, 8, 2)


def number(h, x, y, g):
    return ((h * 4 + x) * 4 + y) * 16 + g


def pairs(to):
    every = [(h, x, y, g) for h in range(2) for x in range(4) for y in range(4) for g in range(16)]
    return [(number(*p), number(*to(*p))) for p in every]


def beside(g):
    return (g + 1) % 16 if g % 2 else (g - 1) % 16


SWAP_A = pairs(lambda h, x, y, g: (h ^ (x % 3 == 0), 3 - x, y, g))
SWAP_B = pairs(lambda h, x, y, g: (h, x ^ 1, y, g))
SWAP_Y = [pairs(lambda h, x, y, g, k=k: (h, x, y ^ k, g)) for k in (1, 2, 3)]
SWAP_E = pairs(lambda h, x, y, g: (h, x, y, g ^ 1))
SWAP_O = pairs(lambda h, x, y, g: (h, x, y, beside(g)))
SWAP_AO = pairs(lambda h, x, y, g: (h ^ (x % 3 == 0), 3 - x, y, beside(g)))


def send(x, perm):
    return lax.ppermute(x, AXES, perm)


def put_main(field, block, main):
    field[block, :, :, YREACH:YREACH + ROWS, :] = main[...].astype(jnp.float32)


def put_halo(field, block, even, odd):
    c = lax.axis_index("c")

    @pl.when(c == 0)
    def _():
        field[block, :, :, 0:YREACH, :] = odd[...].astype(jnp.float32)
        field[block, :, :, YREACH + ROWS:, :] = even[...].astype(jnp.float32)

    @pl.when(c == 1)
    def _():
        field[block, :, :, 0:YREACH, :] = even[...].astype(jnp.float32)
        field[block, :, :, YREACH + ROWS:, :] = odd[...].astype(jnp.float32)


def list_planes(lag_ref, items, own):
    y = lax.axis_index("y")
    odd_x = lax.axis_index("x") & 1
    sink = (1 if own else 3) << 15
    items[0] = sink

    def segment(n, used):
        lag = n >> 1
        second = n & 1
        lag_z = lag_ref[lag, 2]
        rest = lag_z & (PLANES - 1)
        hops = (lag_z >> 4) + 1 - second
        low = jnp.where(second == 1, rest, 0)
        high = jnp.where(second == 1, PLANES, rest)
        target = (y - hops) & 3
        column = (target + hops - y) >> 2
        block = jnp.where(column == 0, 0, jnp.where((column > 0) == (odd_x == 1), 2, 1))
        slot = y ^ target
        high = jnp.where((slot == 0) == own, high, low)
        into = 0 if own else slot - 1
        fixed = (block << 4) | (lag << 6) | (into << 13) | (into << 15)

        def note(plane, used):
            items[used] = fixed | plane | (((plane - rest) & (PLANES - 1)) << 9)
            return used + 1

        return lax.fori_loop(low, high, note, used)

    used = lax.fori_loop(0, 2 * NLAG, segment, jnp.int32(1))
    for extra in range(3):
        items[used + extra] = sink
    return used - 1


def add_planes(lag_ref, field, base, gains, sums, items, turned0, turned1, parts0, parts1, own):
    count = list_planes(lag_ref, items, own)

    def turn(item, turned):
        plane = item & 15
        block = (item >> 4) & 3
        lag = (item >> 6) & 7
        at = (item >> 9) & 15
        slot = (item >> 13) & 3
        start = lag_ref[lag, 0]
        first = YREACH + lag_ref[lag, 1]
        for c in range(3):
            wide = base[slot, c, at].astype(jnp.float32)
            for h in range(2):
                moved = field[block, c, plane, pl.ds(first + 8 * h, 8), :]
                for i in range(4):
                    shift = (2 * LANES - start - 4 * i) & (LANES - 1)
                    turned[h, i, c] = pltpu.roll(moved, shift, 1)
                here = wide[8 * h:8 * h + 8]
                for j in range(4):
                    turned[h, 4 + j, c] = pltpu.roll(here, j, 1) if j else here

    def add(item, turned, parts):
        gain = ((item >> 6) & 7) * NOFF
        for h in range(2):
            for j in range(4):
                here = [turned[h, 4 + j, c] for c in range(3)]
                part = None
                for i in range(4):
                    g0, g1, g2 = (gains[gain + 4 * i + j, c] for c in range(3))
                    d0, d1, d2 = (turned[h, i, c] - here[c] for c in range(3))
                    along = g0 * d0 + g1 * d1 + g2 * d2
                    energy = d0 * d0 + d1 * d1 + d2 * d2
                    term = along * energy
                    part = term if part is None else part + term
                parts[h, j] = part

    def finish(item, parts):
        at = (item >> 9) & 15
        into = (item >> 15) & 3
        for h in range(2):
            total = sums[into, at, 8 * h:8 * h + 8, :] + parts[h, 0]
            for j in range(1, 4):
                total = total + pltpu.roll(parts[h, j], LANES - j, 1)
            sums[into, at, 8 * h:8 * h + 8, :] = total

    def two(i, carry):
        before, here, there, after = (items[2 * i + n] for n in range(4))
        add(here, turned0, parts0)
        turn(there, turned1)
        finish(before, parts1)
        add(there, turned1, parts1)
        turn(after, turned0)
        finish(here, parts0)
        return carry

    steps = (count + 1) >> 1
    parts1[...] = jnp.zeros_like(parts1)
    turn(items[1], turned0)
    lax.fori_loop(0, steps, two, 0)
    finish(items[2 * steps], parts1)


def prepare(index_ref, weight_ref, u_ref, b_ref, field, gains):
    def fill(lag, carry):
        for k in range(NOFF):
            row = index_ref[lag, k]
            for c in range(3):
                gains[lag * NOFF + k, c] = jnp.full((8, LANES), weight_ref[c, row], jnp.float32)
        return carry

    lax.fori_loop(0, NLAG, fill, 0)
    put_main(field, 0, u_ref)
    put_main(field, 1, b_ref)


def others(
    lag_ref, field_in, gains, a_ref, e_ref, o_ref, ao_ref, r1_ref, r2_ref, r3_ref,
    field, out1, out2, out3, base, sums, *work,
):
    del field_in
    put_main(field, 2, a_ref)
    put_halo(field, 0, e_ref.at[0], o_ref.at[0])
    put_halo(field, 1, e_ref.at[1], o_ref.at[1])
    put_halo(field, 2, e_ref.at[2], ao_ref)
    for slot, ref in enumerate((r1_ref, r2_ref, r3_ref)):
        base[slot] = ref[...]
    sums[...] = jnp.zeros_like(sums)
    add_planes(lag_ref, field, base, gains, sums, *work, False)
    for slot, ref in enumerate((out1, out2, out3)):
        ref[...] = sums[slot]


def selves(lag_ref, field, gains, u_ref, out, sums, *work):
    sums[...] = jnp.zeros_like(sums)
    add_planes(lag_ref, field, u_ref, gains, sums, *work, True)
    out[...] = sums[0]


WORK = [
    pltpu.SMEM((NLAG * PLANES + 4,), jnp.int32),
    pltpu.VMEM((2, 8, 3, 8, LANES), jnp.float32),
    pltpu.VMEM((2, 8, 3, 8, LANES), jnp.float32),
    pltpu.VMEM((2, 4, 8, LANES), jnp.float32),
    pltpu.VMEM((2, 4, 8, LANES), jnp.float32),
]
FIELD = jax.ShapeDtypeStruct((3, 3, PLANES, ROWS + 2 * YREACH, LANES), jnp.float32)
GAINS = jax.ShapeDtypeStruct((NLAG * NOFF, 3, 8, LANES), jnp.float32)
PART = jax.ShapeDtypeStruct((PLANES, ROWS, LANES), jnp.float32)


def call(kernel, scalars, fields, outs, flops, scratch=(), aliases=None):
    smem = pl.BlockSpec(memory_space=pltpu.SMEM)
    vmem = pl.BlockSpec(memory_space=pltpu.VMEM)
    return pl.pallas_call(
        kernel,
        out_shape=outs,
        in_specs=[smem] * len(scalars) + [vmem] * len(fields),
        out_specs=jax.tree.map(lambda _: vmem, outs),
        scratch_shapes=scratch,
        input_output_aliases=aliases or {},
        cost_estimate=pl.CostEstimate(flops=flops, bytes_accessed=4 << 20, transcendentals=0),
        compiler_params=pltpu.CompilerParams(vmem_limit_bytes=12 << 20),
    )(*scalars, *fields)


def per_device(velocity, lag_table, filter_index, filter_weights):
    c = lax.axis_index("c")

    def edge(x, upper):
        low = x[..., :YREACH, :]
        high = x[..., ROWS - YREACH:, :]
        return jnp.where(c == upper, high, low)

    a = send(velocity, SWAP_A)
    ao = send(edge(velocity, 1), SWAP_AO)
    b = send(velocity, SWAP_B)
    r1, r2, r3 = (send(velocity, perm) for perm in SWAP_Y)
    o = send(edge(jnp.stack([velocity, b]), 1), SWAP_O)
    field, gains = call(
        prepare, (filter_index, filter_weights), (velocity, b), (FIELD, GAINS), 1 << 21
    )
    trio = jnp.stack(lax.optimization_barrier((velocity, b, a)))
    e = send(edge(trio, 0), SWAP_E)
    field, s1, s2, s3 = call(
        others, (lag_table,), (field, gains, a, e, o, ao, r1, r2, r3),
        (FIELD, PART, PART, PART), 3 << 23,
        [pltpu.VMEM((3, 3, PLANES, ROWS, LANES), jnp.bfloat16),
         pltpu.VMEM((4, PLANES, ROWS, LANES), jnp.float32), *WORK], {1: 0},
    )
    p1, p2, p3 = (send(s, perm) for s, perm in zip((s1, s2, s3), SWAP_Y))
    own = call(
        selves, (lag_table,), (field, gains, velocity[None]), PART, 3 << 23,
        [pltpu.VMEM((2, PLANES, ROWS, LANES), jnp.float32), *WORK],
    )
    return (own + p1 + p2 + p3) * (0.25 / (NLAG * NOFF))


def solution(mesh):
    inner = Mesh(mesh.devices.reshape(SIZES), AXES)
    in_specs = (P(None, ("zh", "x", "y"), ("zl", "c"), None), P(), P(), P())
    out_specs = P(("zh", "x", "y"), ("zl", "c"), None)
    return jax.shard_map(
        per_device, mesh=inner, in_specs=in_specs, out_specs=out_specs, check_vma=False
    )
```

time: 86.9 us -> 90.7 us (1.044)
  the two profiles are of different devices: /device:TPU:8 before, /device:TPU:24 now
where the time goes in v2:
time: 90.7 us; the launch traced here: 90.1 us
  starting transfers between devices  59.6 us (66%)
  waiting for transfers between devices  12.4 us (14%)
  Pallas kernels  11.1 us (12%)
  other arithmetic  3.77 us (4%)
  local copies, waits for them, and re-layouts  3.06 us (3%)
    ppermute x11, starting transfers between devices, send(): return lax.ppermute(x, AXES, perm)  59.6 us
    ppermute x11, waiting for transfers between devices, send(): return lax.ppermute(x, AXES, perm)  12.4 us
    pallas_call x3, Pallas kernels, call(): pl.pallas_call(kernel, out_shape=outs, in_specs=[smem] * len(scalars) + [...  11.1 us
    select_n x3, other arithmetic, edge(): return jnp.where(c == upper, high, low)  3.07 us
    unnamed x7, local copies, waits for them, and re-layouts  3.06 us
  transfers between devices with their start and end apart: 11, of which 2 were waited for; matrix products, arithmetic and copies ran while one was open for 4% of the time, Pallas kernels for 7%

profile of v2, /device:TPU:24, one launch (start us, length us, event | category | flops | bytes accessed | tf_op | source)
XLA Modules:
  0.0 90.1 jit_solution(15122932533441835865)
XLA Ops:
  0.0 2.6 %collective-permute-start.5 = (bf16[3,16,16,128]{3,2,1,0:T(8,128)(2,1)}, bf16[3,16,16,128]{3,2,1,0:T(8,128)(2,1)S(1)}, u32[]{:S(2)}, u32[]{:S(2)}) collective-permute-start(bf16[3,16,16,128]{3,2,1,0:T(8,128)(2,1)} %u_ref.1), channel_id=1, source_target_pairs={{0,16},{1,17},{2,18},{3,19},{4,20},{5,21},{6,22},{7,23},{8,24},{9,... | collective-permute-start | bytes 589832 | tf_op jit(solution)/shard_map/ppermute | solution.py:42
  2.6 17.9 %collective-permute-start.1 = (bf16[3,16,16,128]{3,2,1,0:T(8,128)(2,1)}, bf16[3,16,16,128]{3,2,1,0:T(8,128)(2,1)S(1)}, u32[]{:S(2)}, u32[]{:S(2)}) collective-permute-start(bf16[3,16,16,128]{3,2,1,0:T(8,128)(2,1)} %u_ref.1), channel_id=1, source_target_pairs={{0,448},{1,449},{2,450},{3,451},{4,452},{5,453},{6,454},{7,455},{8... | collective-permute-start | bytes 589832 | tf_op jit(solution)/shard_map/ppermute | solution.py:42
  20.6 1.9 %collective-permute-start = (bf16[3,16,16,128]{3,2,1,0:T(8,128)(2,1)}, bf16[3,16,16,128]{3,2,1,0:T(8,128)(2,1)S(1)}, u32[]{:S(2)}, u32[]{:S(2)}) collective-permute-start(bf16[3,16,16,128]{3,2,1,0:T(8,128)(2,1)} %u_ref.1), channel_id=1, source_target_pairs={{0,64},{1,65},{2,66},{3,67},{4,68},{5,69},{6,70},{7,71},{8,72},{9,... | collective-permute-start | bytes 589832 | tf_op jit(solution)/shard_map/ppermute | solution.py:42
  22.5 3.0 %collective-permute-start.7 = (bf16[3,16,16,128]{3,2,1,0:T(8,128)(2,1)}, bf16[3,16,16,128]{3,2,1,0:T(8,128)(2,1)S(1)}, u32[]{:S(2)}, u32[]{:S(2)}) collective-permute-start(bf16[3,16,16,128]{3,2,1,0:T(8,128)(2,1)} %u_ref.1), channel_id=1, source_target_pairs={{0,48},{1,49},{2,50},{3,51},{4,52},{5,53},{6,54},{7,55},{8,56},{9,... | collective-permute-start | bytes 589832 | tf_op jit(solution)/shard_map/ppermute | solution.py:42
  25.5 4.2 %collective-permute-start.6 = (bf16[3,16,16,128]{3,2,1,0:T(8,128)(2,1)}, bf16[3,16,16,128]{3,2,1,0:T(8,128)(2,1)S(1)}, u32[]{:S(2)}, u32[]{:S(2)}) collective-permute-start(bf16[3,16,16,128]{3,2,1,0:T(8,128)(2,1)} %u_ref.1), channel_id=1, source_target_pairs={{0,32},{1,33},{2,34},{3,35},{4,36},{5,37},{6,38},{7,39},{8,40},{9,... | collective-permute-start | bytes 589832 | tf_op jit(solution)/shard_map/ppermute | solution.py:42
  29.7 1.0 %slice_select_fusion = bf16[3,16,4,128]{3,2,1,0:T(4,128)(2,1)S(1)} fusion(bf16[3,16,16,128]{3,2,1,0:T(8,128)(2,1)} %u_ref.1, pred[]{:T(512)S(6)} %eq.8), kind=kLoop, calls=%fused_computation.6 | loop fusion | flops 24576 | bytes 147457 | tf_op jit(solution)/shard_map/jit(_where)/select_n | solution.py:229
  30.7 6.2 %collective-permute-done.1.a_ref = bf16[3,16,16,128]{3,2,1,0:T(8,128)(2,1)S(1)} collective-permute-done((bf16[3,16,16,128]{3,2,1,0:T(8,128)(2,1)}, bf16[3,16,16,128]{3,2,1,0:T(8,128)(2,1)S(1)}, u32[]{:S(2)}, u32[]{:S(2)}) %collective-permute-start.1) | collective-permute-done | bytes 196640 | tf_op jit(solution)/shard_map/ppermute | solution.py:42
  36.8 4.4 %collective-permute-start.4 = (bf16[3,16,4,128]{3,2,1,0:T(4,128)(2,1)S(1)}, bf16[3,16,4,128]{3,2,1,0:T(4,128)(2,1)S(1)}, u32[]{:S(2)}, u32[]{:S(2)}) collective-permute-start(bf16[3,16,4,128]{3,2,1,0:T(4,128)(2,1)S(1)} %slice_select_fusion), channel_id=1, source_target_pairs={{0,463},{1,450},{2,449},{3,452},{4,451},{5,454},{6,453},{7,456},{8... | collective-permute-start | bytes 147464 | tf_op jit(solution)/shard_map/ppermute | solution.py:42
  41.2 0.0 collective-permute-done.b_ref
  41.3 1.1 %fusion = bf16[3,3,16,4,128]{4,3,2,1,0:T(4,128)(2,1)S(1)} fusion(bf16[1,3,16,16,128]{4,3,2,1,0:T(8,128)(2,1)S(1)} %bitcast.10, bf16[1,3,16,16,128]{4,3,2,1,0:T(8,128)(2,1)S(1)} %bitcast.8, bf16[1,3,16,16,128]{4,3,2,1,0:T(8,128)(2,1)} %bitcast.5, pred[]{:T(512)S(6)} %eq.7), kind=kLoop, calls=%fused_computation.1 | loop fusion | flops 958464 | bytes 737281 | tf_op jit(solution)/shard_map/jit(_where)/select_n | solution.py:229
  42.3 12.9 %collective-permute-start.2 = (bf16[3,3,16,4,128]{4,3,2,1,0:T(4,128)(2,1)S(1)}, bf16[3,3,16,4,128]{4,3,2,1,0:T(4,128)(2,1)S(1)}, u32[]{:S(2)}, u32[]{:S(2)}) collective-permute-start(bf16[3,3,16,4,128]{4,3,2,1,0:T(4,128)(2,1)S(1)} %fusion), channel_id=1, source_target_pairs={{0,1},{1,0},{2,3},{3,2},{4,5},{5,4},{6,7},{7,6},{8,9},{9,8},{10,11... | collective-permute-start | bytes 442376 | tf_op jit(solution)/shard_map/ppermute | solution.py:42
  55.2 1.0 %fusion.1 = bf16[2,3,16,4,128]{4,3,2,1,0:T(4,128)(2,1)S(1)} fusion(bf16[1,3,16,16,128]{4,3,2,1,0:T(8,128)(2,1)S(1)} %bitcast.9, bf16[1,3,16,16,128]{4,3,2,1,0:T(8,128)(2,1)} %bitcast.6, pred[]{:T(512)S(6)} %eq.8), kind=kLoop, calls=%fused_computation.5 | loop fusion | flops 442368 | bytes 491521 | tf_op jit(solution)/shard_map/jit(_where)/select_n | solution.py:229
  56.2 0.0 collective-permute-done.4.ao_ref
  56.3 2.2 %collective-permute-start.3 = (bf16[2,3,16,4,128]{4,3,2,1,0:T(4,128)(2,1)S(1)}, bf16[2,3,16,4,128]{4,3,2,1,0:T(4,128)(2,1)S(1)}, u32[]{:S(2)}, u32[]{:S(2)}) collective-permute-start(bf16[2,3,16,4,128]{4,3,2,1,0:T(4,128)(2,1)S(1)} %fusion.1), channel_id=1, source_target_pairs={{0,15},{1,2},{2,1},{3,4},{4,3},{5,6},{6,5},{7,8},{8,7},{9,10},{10,... | collective-permute-start | bytes 294920 | tf_op jit(solution)/shard_map/ppermute | solution.py:42
  58.5 0.8 copy.7.lag_ref
  59.3 0.0 copy-start
  59.3 0.9 %copy-done = bf16[3,16,16,128]{3,2,1,0:T(8,128)(2,1)S(1)} copy-done((bf16[3,16,16,128]{3,2,1,0:T(8,128)(2,1)S(1)}, bf16[3,16,16,128]{3,2,1,0:T(8,128)(2,1)}, u32[]{:S(2)}) %copy-start) | copy-done | bytes 196632
  60.2 0.0 copy-start.1
  60.2 0.7 copy-done.1
  60.9 0.0 copy-start.2
  60.9 0.7 copy-done.2
  61.6 0.9 %shard_map.46 = (f32[3,3,16,24,128]{4,3,2,1,0:T(8,128)S(1)}, f32[80,3,8,128]{3,2,1,0:T(8,128)S(1)}) custom-call(s32[5,16]{1,0:T(8,128)S(1)} %copy-done.1, f32[3,32]{1,0:T(4,128)S(1)} %copy-done.2, bf16[3,16,16,128]{3,2,1,0:T(8,128)(2,1)S(1)} %copy-done, bf16[3,16,16,128]{3,2,1,0:T(8,128)(2,1)S(1)} %collective-permute-done.b_ref), custom_call_target="tpu_custom_call" | custom-call | flops 2097152 | bytes 4194304 | tf_op jit(solution)/shard_map/pallas_call | solution.py:211
  62.5 0.0 collective-permute-done.5.r1_ref
  62.5 0.0 collective-permute-done.7.r3_ref
  62.5 0.0 collective-permute-done.6.r2_ref
  62.5 6.2 %collective-permute-done.3.o_ref = bf16[2,3,16,4,128]{4,3,2,1,0:T(4,128)(2,1)S(1)} collective-permute-done((bf16[2,3,16,4,128]{4,3,2,1,0:T(4,128)(2,1)S(1)}, bf16[2,3,16,4,128]{4,3,2,1,0:T(4,128)(2,1)S(1)}, u32[]{:S(2)}, u32[]{:S(2)}) %collective-permute-start.3) | collective-permute-done | bytes 98336 | tf_op jit(solution)/shard_map/ppermute | solution.py:42
  68.8 0.0 collective-permute-done.2.e_ref
  68.8 5.0 %shard_map.47 = (f32[3,3,16,24,128]{4,3,2,1,0:T(8,128)S(1)}, f32[16,16,128]{2,1,0:T(8,128)S(1)}, f32[16,16,128]{2,1,0:T(8,128)S(1)}, f32[16,16,128]{2,1,0:T(8,128)S(1)}) custom-call(s32[5,3]{1,0:T(8,128)S(1)} %copy.7.lag_ref, f32[3,3,16,24,128]{4,3,2,1,0:T(8,128)S(1)} %get-tuple-element.14.field_in, ...), custom_call_target="tpu_custom_call", output_to_operand_aliasing={{0}: (1, {})} | custom-call | flops 25165824 | bytes 4194304 | tf_op jit(solution)/shard_map/pallas_call | solution.py:211
  73.8 3.2 %collective-permute-start.8 = (f32[16,16,128]{2,1,0:T(8,128)S(1)}, f32[16,16,128]{2,1,0:T(8,128)S(1)}, u32[]{:S(2)}, u32[]{:S(2)}) collective-permute-start(f32[16,16,128]{2,1,0:T(8,128)S(1)} %get-tuple-element.20), channel_id=1, source_target_pairs={{0,16},{1,17},{2,18},{3,19},{4,20},{5,21},{6,22},{7,23},{8,24},{9,... | collective-permute-start | bytes 393224 | tf_op jit(solution)/shard_map/ppermute | solution.py:42
  77.0 3.1 %collective-permute-start.9 = (f32[16,16,128]{2,1,0:T(8,128)S(1)}, f32[16,16,128]{2,1,0:T(8,128)S(1)}, u32[]{:S(2)}, u32[]{:S(2)}) collective-permute-start(f32[16,16,128]{2,1,0:T(8,128)S(1)} %get-tuple-element.21), channel_id=1, source_target_pairs={{0,32},{1,33},{2,34},{3,35},{4,36},{5,37},{6,38},{7,39},{8,40},{9,... | collective-permute-start | bytes 393224 | tf_op jit(solution)/shard_map/ppermute | solution.py:42
  80.1 4.1 %collective-permute-start.10 = (f32[16,16,128]{2,1,0:T(8,128)S(1)}, f32[16,16,128]{2,1,0:T(8,128)S(1)}, u32[]{:S(2)}, u32[]{:S(2)}) collective-permute-start(f32[16,16,128]{2,1,0:T(8,128)S(1)} %get-tuple-element.22), channel_id=1, source_target_pairs={{0,48},{1,49},{2,50},{3,51},{4,52},{5,53},{6,54},{7,55},{8,56},{9,... | collective-permute-start | bytes 393224 | tf_op jit(solution)/shard_map/ppermute | solution.py:42
  84.2 5.2 %shard_map.48 = f32[16,16,128]{2,1,0:T(8,128)S(1)} custom-call(s32[5,3]{1,0:T(8,128)S(1)} %copy.7.lag_ref, f32[3,3,16,24,128]{4,3,2,1,0:T(8,128)S(1)} %get-tuple-element.19.field, f32[80,3,8,128]{3,2,1,0:T(8,128)S(1)} %get-tuple-element.15.gains, bf16[1,3,16,16,128]{4,3,2,1,0:T(8,128)(2,1)S(1)} %bitcast.7), custom_call_target="tpu_custom_call" | custom-call | flops 25165824 | bytes 4194304 | tf_op jit(solution)/shard_map/pallas_call | solution.py:211
  89.4 0.0 collective-permute-done.8
  89.4 0.0 collective-permute-done.9
  89.4 0.0 collective-permute-done.10
  89.4 0.7 add_multiply_fusion
Async XLA Ops:
  0.0 62.5 %collective-permute-start.5 = (bf16[3,16,16,128]{3,2,1,0:T(8,128)(2,1)}, bf16[3,16,16,128]{3,2,1,0:T(8,128)(2,1)S(1)}, u32[]{:S(2)}, u32[]{:S(2)}) collective-permute-start(bf16[3,16,16,128]{3,2,1,0:T(8,128)(2,1)} %u_ref.1), channel_id=1, source_target_pairs={{0,16},{1,17},{2,18},{3,19},{4,20},{5,21},{6,22},{7,23},{8,24},{9,... | collective-permute-start | bytes 589832 | tf_op jit(solution)/shard_map/ppermute | solution.py:42
  2.6 34.2 %collective-permute-start.1 = (bf16[3,16,16,128]{3,2,1,0:T(8,128)(2,1)}, bf16[3,16,16,128]{3,2,1,0:T(8,128)(2,1)S(1)}, u32[]{:S(2)}, u32[]{:S(2)}) collective-permute-start(bf16[3,16,16,128]{3,2,1,0:T(8,128)(2,1)} %u_ref.1), channel_id=1, source_target_pairs={{0,448},{1,449},{2,450},{3,451},{4,452},{5,453},{6,454},{7,455},{8... | collective-permute-start | bytes 589832 | tf_op jit(solution)/shard_map/ppermute | solution.py:42
  20.6 20.7 %collective-permute-start = (bf16[3,16,16,128]{3,2,1,0:T(8,128)(2,1)}, bf16[3,16,16,128]{3,2,1,0:T(8,128)(2,1)S(1)}, u32[]{:S(2)}, u32[]{:S(2)}) collective-permute-start(bf16[3,16,16,128]{3,2,1,0:T(8,128)(2,1)} %u_ref.1), channel_id=1, source_target_pairs={{0,64},{1,65},{2,66},{3,67},{4,68},{5,69},{6,70},{7,71},{8,72},{9,... | collective-permute-start | bytes 589832 | tf_op jit(solution)/shard_map/ppermute | solution.py:42
  22.5 40.0 %collective-permute-start.7 = (bf16[3,16,16,128]{3,2,1,0:T(8,128)(2,1)}, bf16[3,16,16,128]{3,2,1,0:T(8,128)(2,1)S(1)}, u32[]{:S(2)}, u32[]{:S(2)}) collective-permute-start(bf16[3,16,16,128]{3,2,1,0:T(8,128)(2,1)} %u_ref.1), channel_id=1, source_target_pairs={{0,48},{1,49},{2,50},{3,51},{4,52},{5,53},{6,54},{7,55},{8,56},{9,... | collective-permute-start | bytes 589832 | tf_op jit(solution)/shard_map/ppermute | solution.py:42
  25.5 37.1 %collective-permute-start.6 = (bf16[3,16,16,128]{3,2,1,0:T(8,128)(2,1)}, bf16[3,16,16,128]{3,2,1,0:T(8,128)(2,1)S(1)}, u32[]{:S(2)}, u32[]{:S(2)}) collective-permute-start(bf16[3,16,16,128]{3,2,1,0:T(8,128)(2,1)} %u_ref.1), channel_id=1, source_target_pairs={{0,32},{1,33},{2,34},{3,35},{4,36},{5,37},{6,38},{7,39},{8,40},{9,... | collective-permute-start | bytes 589832 | tf_op jit(solution)/shard_map/ppermute | solution.py:42
  36.8 19.4 %collective-permute-start.4 = (bf16[3,16,4,128]{3,2,1,0:T(4,128)(2,1)S(1)}, bf16[3,16,4,128]{3,2,1,0:T(4,128)(2,1)S(1)}, u32[]{:S(2)}, u32[]{:S(2)}) collective-permute-start(bf16[3,16,4,128]{3,2,1,0:T(4,128)(2,1)S(1)} %slice_select_fusion), channel_id=1, source_target_pairs={{0,463},{1,450},{2,449},{3,452},{4,451},{5,454},{6,453},{7,456},{8... | collective-permute-start | bytes 147464 | tf_op jit(solution)/shard_map/ppermute | solution.py:42
  42.3 26.5 %collective-permute-start.2 = (bf16[3,3,16,4,128]{4,3,2,1,0:T(4,128)(2,1)S(1)}, bf16[3,3,16,4,128]{4,3,2,1,0:T(4,128)(2,1)S(1)}, u32[]{:S(2)}, u32[]{:S(2)}) collective-permute-start(bf16[3,3,16,4,128]{4,3,2,1,0:T(4,128)(2,1)S(1)} %fusion), channel_id=1, source_target_pairs={{0,1},{1,0},{2,3},{3,2},{4,5},{5,4},{6,7},{7,6},{8,9},{9,8},{10,11... | collective-permute-start | bytes 442376 | tf_op jit(solution)/shard_map/ppermute | solution.py:42
  56.3 12.5 %collective-permute-start.3 = (bf16[2,3,16,4,128]{4,3,2,1,0:T(4,128)(2,1)S(1)}, bf16[2,3,16,4,128]{4,3,2,1,0:T(4,128)(2,1)S(1)}, u32[]{:S(2)}, u32[]{:S(2)}) collective-permute-start(bf16[2,3,16,4,128]{4,3,2,1,0:T(4,128)(2,1)S(1)} %fusion.1), channel_id=1, source_target_pairs={{0,15},{1,2},{2,1},{3,4},{4,3},{5,6},{6,5},{7,8},{8,7},{9,10},{10,... | collective-permute-start | bytes 294920 | tf_op jit(solution)/shard_map/ppermute | solution.py:42
  59.3 0.9 %copy-start = (bf16[3,16,16,128]{3,2,1,0:T(8,128)(2,1)S(1)}, bf16[3,16,16,128]{3,2,1,0:T(8,128)(2,1)}, u32[]{:S(2)}) copy-start(bf16[3,16,16,128]{3,2,1,0:T(8,128)(2,1)} %u_ref.1) | copy-start | bytes 589828
  60.2 0.7 copy-start.1
  60.9 0.7 copy-start.2
  73.8 15.6 %collective-permute-start.8 = (f32[16,16,128]{2,1,0:T(8,128)S(1)}, f32[16,16,128]{2,1,0:T(8,128)S(1)}, u32[]{:S(2)}, u32[]{:S(2)}) collective-permute-start(f32[16,16,128]{2,1,0:T(8,128)S(1)} %get-tuple-element.20), channel_id=1, source_target_pairs={{0,16},{1,17},{2,18},{3,19},{4,20},{5,21},{6,22},{7,23},{8,24},{9,... | collective-permute-start | bytes 393224 | tf_op jit(solution)/shard_map/ppermute | solution.py:42
  77.0 12.4 %collective-permute-start.9 = (f32[16,16,128]{2,1,0:T(8,128)S(1)}, f32[16,16,128]{2,1,0:T(8,128)S(1)}, u32[]{:S(2)}, u32[]{:S(2)}) collective-permute-start(f32[16,16,128]{2,1,0:T(8,128)S(1)} %get-tuple-element.21), channel_id=1, source_target_pairs={{0,32},{1,33},{2,34},{3,35},{4,36},{5,37},{6,38},{7,39},{8,40},{9,... | collective-permute-start | bytes 393224 | tf_op jit(solution)/shard_map/ppermute | solution.py:42
  80.1 9.3 %collective-permute-start.10 = (f32[16,16,128]{2,1,0:T(8,128)S(1)}, f32[16,16,128]{2,1,0:T(8,128)S(1)}, u32[]{:S(2)}, u32[]{:S(2)}) collective-permute-start(f32[16,16,128]{2,1,0:T(8,128)S(1)} %get-tuple-element.22), channel_id=1, source_target_pairs={{0,48},{1,49},{2,50},{3,51},{4,52},{5,53},{6,54},{7,55},{8,56},{9,... | collective-permute-start | bytes 393224 | tf_op jit(solution)/shard_map/ppermute | solution.py:42

commit v3 on v2

--- a/solution.py
+++ b/solution.py
@@ -69,7 +69,7 @@
     def segment(n, used):
         lag = n >> 1
         second = n & 1
-        lag_z = lag_ref[lag, 2]
+        lag_z = lag_ref[2, lag]
         rest = lag_z & (PLANES - 1)
         hops = (lag_z >> 4) + 1 - second
         low = jnp.where(second == 1, rest, 0)
@@ -103,8 +103,8 @@
         lag = (item >> 6) & 7
         at = (item >> 9) & 15
         slot = (item >> 13) & 3
-        start = lag_ref[lag, 0]
-        first = YREACH + lag_ref[lag, 1]
+        start = lag_ref[0, lag]
+        first = YREACH + lag_ref[1, lag]
         for c in range(3):
             wide = base[slot, c, at].astype(jnp.float32)
             for h in range(2):
@@ -157,7 +157,41 @@
     finish(items[2 * steps], parts1)
 
 
-def prepare(index_ref, weight_ref, u_ref, b_ref, field, gains):
+def pack(out, refs, upper):
+    c = lax.axis_index("c")
+
+    def take(first):
+        for n, ref in enumerate(refs):
+            for comp in range(3):
+                half = ref[comp, :, 8 * (first // 8):8 * (first // 8) + 8, :].astype(jnp.float32)
+                rows = half[:, first % 8:first % 8 + YREACH, :]
+                out[n, comp] = rows.astype(jnp.bfloat16)
+
+    pl.when(c == upper)(lambda: take(ROWS - YREACH))
+    pl.when(c != upper)(lambda: take(0))
+
+
+def first(u_hbm, u_ref, rows, sem):
+    move = pltpu.make_async_copy(u_hbm, u_ref, sem)
+    move.start()
+    move.wait()
+    pack(rows, (u_ref,), 1)
+
+
+def pair(u_ref, r_ref, both):
+    both[0] = u_ref[...]
+    both[1] = r_ref[...]
+
+
+def second(u_ref, b_ref, rows):
+    pack(rows, (u_ref, b_ref), 1)
+
+
+def third(u_ref, b_ref, a_ref, rows):
+    pack(rows, (u_ref, b_ref, a_ref), 0)
+
+
+def widen(index_ref, weight_ref, u_ref, b_ref, a_ref, field, gains):
     def fill(lag, carry):
         for k in range(NOFF):
             row = index_ref[lag, k]
@@ -166,20 +200,19 @@
         return carry
 
     lax.fori_loop(0, NLAG, fill, 0)
-    put_main(field, 0, u_ref)
-    put_main(field, 1, b_ref)
+    for block, ref in enumerate((u_ref, b_ref, a_ref)):
+        put_main(field, block, ref)
 
 
 def others(
-    lag_ref, field_in, gains, a_ref, e_ref, o_ref, ao_ref, r1_ref, r2_ref, r3_ref,
+    lag_ref, field_in, gains, e_ref, o_ref, ao_ref, r_ref, both_ref,
     field, out1, out2, out3, base, sums, *work,
 ):
     del field_in
-    put_main(field, 2, a_ref)
     put_halo(field, 0, e_ref.at[0], o_ref.at[0])
     put_halo(field, 1, e_ref.at[1], o_ref.at[1])
-    put_halo(field, 2, e_ref.at[2], ao_ref)
-    for slot, ref in enumerate((r1_ref, r2_ref, r3_ref)):
+    put_halo(field, 2, e_ref.at[2], ao_ref.at[0])
+    for slot, ref in enumerate((r_ref, both_ref.at[0], both_ref.at[1])):
         base[slot] = ref[...]
     sums[...] = jnp.zeros_like(sums)
     add_planes(lag_ref, field, base, gains, sums, *work, False)
@@ -201,17 +234,22 @@
     pltpu.VMEM((2, 4, 8, LANES), jnp.float32),
 ]
 FIELD = jax.ShapeDtypeStruct((3, 3, PLANES, ROWS + 2 * YREACH, LANES), jnp.float32)
+BLOCK = jax.ShapeDtypeStruct((3, PLANES, ROWS, LANES), jnp.bfloat16)
 GAINS = jax.ShapeDtypeStruct((NLAG * NOFF, 3, 8, LANES), jnp.float32)
 PART = jax.ShapeDtypeStruct((PLANES, ROWS, LANES), jnp.float32)
 
 
-def call(kernel, scalars, fields, outs, flops, scratch=(), aliases=None):
+def edges(blocks):
+    return jax.ShapeDtypeStruct((blocks, 3, PLANES, YREACH, LANES), jnp.bfloat16)
+
+
+def call(kernel, scalars, fields, outs, flops, scratch=(), aliases=None, space=pltpu.VMEM):
     smem = pl.BlockSpec(memory_space=pltpu.SMEM)
     vmem = pl.BlockSpec(memory_space=pltpu.VMEM)
     return pl.pallas_call(
         kernel,
         out_shape=outs,
-        in_specs=[smem] * len(scalars) + [vmem] * len(fields),
+        in_specs=[smem] * len(scalars) + [pl.BlockSpec(memory_space=space)] * len(fields),
         out_specs=jax.tree.map(lambda _: vmem, outs),
         scratch_shapes=scratch,
         input_output_aliases=aliases or {},
@@ -221,32 +259,29 @@
 
 
 def per_device(velocity, lag_table, filter_index, filter_weights):
-    c = lax.axis_index("c")
-
-    def edge(x, upper):
-        low = x[..., :YREACH, :]
-        high = x[..., ROWS - YREACH:, :]
-        return jnp.where(c == upper, high, low)
-
     a = send(velocity, SWAP_A)
-    ao = send(edge(velocity, 1), SWAP_AO)
     b = send(velocity, SWAP_B)
-    r1, r2, r3 = (send(velocity, perm) for perm in SWAP_Y)
-    o = send(edge(jnp.stack([velocity, b]), 1), SWAP_O)
-    field, gains = call(
-        prepare, (filter_index, filter_weights), (velocity, b), (FIELD, GAINS), 1 << 21
-    )
-    trio = jnp.stack(lax.optimization_barrier((velocity, b, a)))
-    e = send(edge(trio, 0), SWAP_E)
+    u, rows = call(
+        first, (), (velocity,), (BLOCK, edges(1)), 1 << 20, [pltpu.SemaphoreType.DMA],
+        space=pltpu.HBM,
+    )
+    ao = send(rows, SWAP_AO)
+    r = send(velocity, SWAP_Y[0])
+    both = jax.ShapeDtypeStruct((2, *BLOCK.shape), BLOCK.dtype)
+    both = send(call(pair, (), (u, r), both, 1 << 20), SWAP_Y[1])
+    o = send(call(second, (), (u, b), edges(2), 1 << 20), SWAP_O)
+    e = send(call(third, (), (u, b, a), edges(3), 1 << 20), SWAP_E)
+    field, gains = call(widen, (filter_index, filter_weights), (u, b, a), (FIELD, GAINS), 1 << 21)
+    lags = lag_table.T
     field, s1, s2, s3 = call(
-        others, (lag_table,), (field, gains, a, e, o, ao, r1, r2, r3),
+        others, (lags,), (field, gains, e, o, ao, r, both),
         (FIELD, PART, PART, PART), 3 << 23,
         [pltpu.VMEM((3, 3, PLANES, ROWS, LANES), jnp.bfloat16),
          pltpu.VMEM((4, PLANES, ROWS, LANES), jnp.float32), *WORK], {1: 0},
     )
     p1, p2, p3 = (send(s, perm) for s, perm in zip((s1, s2, s3), SWAP_Y))
     own = call(
-        selves, (lag_table,), (field, gains, velocity[None]), PART, 3 << 23,
+        selves, (lags,), (field, gains, u[None]), PART, 3 << 23,
         [pltpu.VMEM((2, PLANES, ROWS, LANES), jnp.float32), *WORK],
     )
     return (own + p1 + p2 + p3) * (0.25 / (NLAG * NOFF))

time: 90.7 us -> 93.9 us (1.035)
  the two profiles are of different devices: /device:TPU:24 before, /device:TPU:1 now
where the time goes in v3:
time: 93.9 us; the launch traced here: 93.5 us
  starting transfers between devices  72.8 us (78%)
  Pallas kernels  11.2 us (12%)
  waiting for transfers between devices  7.68 us (8%)
  local copies, waits for them, and re-layouts  0.94 us (1%)
    ppermute x10, starting transfers between devices, send(): return lax.ppermute(x, AXES, perm)  72.8 us
    pallas_call x7, Pallas kernels, call(): pl.pallas_call(kernel, out_shape=outs, in_specs=[smem] * len(scalars) + [...  11.2 us
    ppermute x10, waiting for transfers between devices, send(): return lax.ppermute(x, AXES, perm)  7.68 us
  transfers between devices with their start and end apart: 10, of which 3 were waited for; matrix products, arithmetic and copies ran while one was open for 0% of the time, Pallas kernels for 7%

profile of v3, /device:TPU:1, one launch (start us, length us, event | category | flops | bytes accessed | tf_op | source)
XLA Modules:
  0.0 93.5 jit_solution(11204872404189179374)
XLA Ops:
  0.0 4.0 %collective-permute-start.5 = (bf16[3,16,16,128]{3,2,1,0:T(8,128)(2,1)}, bf16[3,16,16,128]{3,2,1,0:T(8,128)(2,1)S(1)}, u32[]{:S(2)}, u32[]{:S(2)}) collective-permute-start(bf16[3,16,16,128]{3,2,1,0:T(8,128)(2,1)} %u_hbm.1), channel_id=1, source_target_pairs={{0,16},{1,17},{2,18},{3,19},{4,20},{5,21},{6,22},{7,23},{8,24},{9,... | collective-permute-start | bytes 589832 | tf_op jit(solution)/shard_map/ppermute | solution.py:42
  4.0 0.0 copy-start
  4.0 0.9 copy-done
  5.0 0.0 copy-start.2
  5.0 0.0 copy-start.3
  5.0 0.0 copy-start.1
  5.0 0.3 shard_map.46
  5.3 2.0 %collective-permute-done.5.r_ref = bf16[3,16,16,128]{3,2,1,0:T(8,128)(2,1)S(1)} collective-permute-done((bf16[3,16,16,128]{3,2,1,0:T(8,128)(2,1)}, bf16[3,16,16,128]{3,2,1,0:T(8,128)(2,1)S(1)}, u32[]{:S(2)}, u32[]{:S(2)}) %collective-permute-start.5) | collective-permute-done | bytes 196640 | tf_op jit(solution)/shard_map/ppermute | solution.py:42
  7.3 6.2 %collective-permute-start.6 = (bf16[2,3,16,16,128]{4,3,2,1,0:T(8,128)(2,1)S(1)}, bf16[2,3,16,16,128]{4,3,2,1,0:T(8,128)(2,1)S(1)}, u32[]{:S(2)}, u32[]{:S(2)}) collective-permute-start(bf16[2,3,16,16,128]{4,3,2,1,0:T(8,128)(2,1)S(1)} %shard_map.50), channel_id=1, source_target_pairs={{0,32},{1,33},{2,34},{3,35},{4,36},{5,37},{6,38},{7,39},{8,40},{9,... | collective-permute-start | bytes 1179656 | tf_op jit(solution)/shard_map/ppermute | solution.py:42
  13.6 3.1 %collective-permute-start = (bf16[3,16,16,128]{3,2,1,0:T(8,128)(2,1)S(1)}, bf16[3,16,16,128]{3,2,1,0:T(8,128)(2,1)S(1)}, u32[]{:S(2)}, u32[]{:S(2)}) collective-permute-start(bf16[3,16,16,128]{3,2,1,0:T(8,128)(2,1)S(1)} %copy-done), channel_id=1, source_target_pairs={{0,64},{1,65},{2,66},{3,67},{4,68},{5,69},{6,70},{7,71},{8,72},{9,... | collective-permute-start | bytes 589832 | tf_op jit(solution)/shard_map/ppermute | solution.py:42
  16.7 17.0 %collective-permute-start.1 = (bf16[3,16,16,128]{3,2,1,0:T(8,128)(2,1)S(1)}, bf16[3,16,16,128]{3,2,1,0:T(8,128)(2,1)S(1)}, u32[]{:S(2)}, u32[]{:S(2)}) collective-permute-start(bf16[3,16,16,128]{3,2,1,0:T(8,128)(2,1)S(1)} %copy-done), channel_id=1, source_target_pairs={{0,448},{1,449},{2,450},{3,451},{4,452},{5,453},{6,454},{7,455},{8... | collective-permute-start | bytes 589832 | tf_op jit(solution)/shard_map/ppermute | solution.py:42
  33.7 0.0 collective-permute-done.b_ref
  33.7 3.3 %collective-permute-done.1.a_ref = bf16[3,16,16,128]{3,2,1,0:T(8,128)(2,1)S(1)} collective-permute-done((bf16[3,16,16,128]{3,2,1,0:T(8,128)(2,1)S(1)}, bf16[3,16,16,128]{3,2,1,0:T(8,128)(2,1)S(1)}, u32[]{:S(2)}, u32[]{:S(2)}) %collective-permute-start.1) | collective-permute-done | bytes 196640 | tf_op jit(solution)/shard_map/ppermute | solution.py:42
  37.0 0.1 shard_map.48
  37.1 15.5 %collective-permute-start.2 = (bf16[3,3,16,4,128]{4,3,2,1,0:T(4,128)(2,1)S(1)}, bf16[3,3,16,4,128]{4,3,2,1,0:T(4,128)(2,1)S(1)}, u32[]{:S(2)}, u32[]{:S(2)}) collective-permute-start(bf16[3,3,16,4,128]{4,3,2,1,0:T(4,128)(2,1)S(1)} %shard_map.48), channel_id=1, source_target_pairs={{0,1},{1,0},{2,3},{3,2},{4,5},{5,4},{6,7},{7,6},{8,9},{9,8},{10,11... | collective-permute-start | bytes 442376 | tf_op jit(solution)/shard_map/ppermute | solution.py:42
  52.6 0.1 shard_map.49
  52.6 3.3 %collective-permute-start.3 = (bf16[2,3,16,4,128]{4,3,2,1,0:T(4,128)(2,1)S(1)}, bf16[2,3,16,4,128]{4,3,2,1,0:T(4,128)(2,1)S(1)}, u32[]{:S(2)}, u32[]{:S(2)}) collective-permute-start(bf16[2,3,16,4,128]{4,3,2,1,0:T(4,128)(2,1)S(1)} %shard_map.49), channel_id=1, source_target_pairs={{0,15},{1,2},{2,1},{3,4},{4,3},{5,6},{6,5},{7,8},{8,7},{9,10},{10,... | collective-permute-start | bytes 294920 | tf_op jit(solution)/shard_map/ppermute | solution.py:42
  56.0 14.1 %collective-permute-start.4 = (bf16[1,3,16,4,128]{4,3,2,1,0:T(4,128)(2,1)S(1)}, bf16[1,3,16,4,128]{4,3,2,1,0:T(4,128)(2,1)S(1)}, u32[]{:S(2)}, u32[]{:S(2)}) collective-permute-start(bf16[1,3,16,4,128]{4,3,2,1,0:T(4,128)(2,1)S(1)} %get-tuple-element.16), channel_id=1, source_target_pairs={{0,463},{1,450},{2,449},{3,452},{4,451},{5,454},{6,453},{7,456},{8... | collective-permute-start | bytes 147464 | tf_op jit(solution)/shard_map/ppermute | solution.py:42
  70.1 0.0 copy-done.2
  70.1 0.0 copy-done.3
  70.1 1.0 %shard_map.47 = (f32[3,3,16,24,128]{4,3,2,1,0:T(8,128)S(1)}, f32[80,3,8,128]{3,2,1,0:T(8,128)S(1)}) custom-call(s32[5,16]{1,0:T(8,128)S(1)} %copy-done.2, f32[3,32]{1,0:T(4,128)S(1)} %copy-done.3, bf16[3,16,16,128]{3,2,1,0:T(8,128)(2,1)S(1)} %get-tuple-element.13.u_ref, bf16[3,16,16,128]{3,2,1,0:T(8,128)(2,1)S(1)} %collective-permute-done.b_ref, ...), custom_call_target="tpu_custom_call" | custom-call | flops 2097152 | bytes 4194304 | tf_op jit(solution)/shard_map/pallas_call | solution.py:249
  71.0 2.3 %collective-permute-done.4.ao_ref = bf16[1,3,16,4,128]{4,3,2,1,0:T(4,128)(2,1)S(1)} collective-permute-done((bf16[1,3,16,4,128]{4,3,2,1,0:T(4,128)(2,1)S(1)}, bf16[1,3,16,4,128]{4,3,2,1,0:T(4,128)(2,1)S(1)}, u32[]{:S(2)}, u32[]{:S(2)}) %collective-permute-start.4) | collective-permute-done | bytes 49184 | tf_op jit(solution)/shard_map/ppermute | solution.py:42
  73.4 0.0 collective-permute-done.3.o_ref
  73.4 0.0 collective-permute-done.2.e_ref
  73.4 0.0 collective-permute-done.6.both_ref
  73.4 0.0 copy-done.1
  73.4 4.8 %shard_map.51 = (f32[3,3,16,24,128]{4,3,2,1,0:T(8,128)S(1)}, f32[16,16,128]{2,1,0:T(8,128)S(1)}, f32[16,16,128]{2,1,0:T(8,128)S(1)}, f32[16,16,128]{2,1,0:T(8,128)S(1)}) custom-call(s32[3,5]{1,0:T(4,128)S(1)} %bitcast.3, f32[3,3,16,24,128]{4,3,2,1,0:T(8,128)S(1)} %get-tuple-element.14.field_in, ...), custom_call_target="tpu_custom_call", output_to_operand_aliasing={{0}: (1, {})} | custom-call | flops 25165824 | bytes 4194304 | tf_op jit(solution)/shard_map/pallas_call | solution.py:249
  78.2 2.3 %collective-permute-start.7 = (f32[16,16,128]{2,1,0:T(8,128)S(1)}, f32[16,16,128]{2,1,0:T(8,128)S(1)}, u32[]{:S(2)}, u32[]{:S(2)}) collective-permute-start(f32[16,16,128]{2,1,0:T(8,128)S(1)} %get-tuple-element.18), channel_id=1, source_target_pairs={{0,16},{1,17},{2,18},{3,19},{4,20},{5,21},{6,22},{7,23},{8,24},{9,... | collective-permute-start | bytes 393224 | tf_op jit(solution)/shard_map/ppermute | solution.py:42
  80.5 3.5 %collective-permute-start.8 = (f32[16,16,128]{2,1,0:T(8,128)S(1)}, f32[16,16,128]{2,1,0:T(8,128)S(1)}, u32[]{:S(2)}, u32[]{:S(2)}) collective-permute-start(f32[16,16,128]{2,1,0:T(8,128)S(1)} %get-tuple-element.19), channel_id=1, source_target_pairs={{0,32},{1,33},{2,34},{3,35},{4,36},{5,37},{6,38},{7,39},{8,40},{9,... | collective-permute-start | bytes 393224 | tf_op jit(solution)/shard_map/ppermute | solution.py:42
  84.0 3.8 %collective-permute-start.9 = (f32[16,16,128]{2,1,0:T(8,128)S(1)}, f32[16,16,128]{2,1,0:T(8,128)S(1)}, u32[]{:S(2)}, u32[]{:S(2)}) collective-permute-start(f32[16,16,128]{2,1,0:T(8,128)S(1)} %get-tuple-element.20), channel_id=1, source_target_pairs={{0,48},{1,49},{2,50},{3,51},{4,52},{5,53},{6,54},{7,55},{8,56},{9,... | collective-permute-start | bytes 393224 | tf_op jit(solution)/shard_map/ppermute | solution.py:42
  87.8 5.0 %shard_map.52 = f32[16,16,128]{2,1,0:T(8,128)S(1)} custom-call(s32[3,5]{1,0:T(4,128)S(1)} %bitcast.4, f32[3,3,16,24,128]{4,3,2,1,0:T(8,128)S(1)} %get-tuple-element.17.field, f32[80,3,8,128]{3,2,1,0:T(8,128)S(1)} %get-tuple-element.15.gains, bf16[1,3,16,16,128]{4,3,2,1,0:T(8,128)(2,1)S(1)} %bitcast.2), custom_call_target="tpu_custom_call" | custom-call | flops 25165824 | bytes 4194304 | tf_op jit(solution)/shard_map/pallas_call | solution.py:249
  92.8 0.0 collective-permute-done.7
  92.8 0.0 collective-permute-done.8
  92.8 0.0 collective-permute-done.9
  92.9 0.7 add_multiply_fusion
  (1 shorter events, 0.0 us)
Async XLA Ops:
  0.0 7.3 %collective-permute-start.5 = (bf16[3,16,16,128]{3,2,1,0:T(8,128)(2,1)}, bf16[3,16,16,128]{3,2,1,0:T(8,128)(2,1)S(1)}, u32[]{:S(2)}, u32[]{:S(2)}) collective-permute-start(bf16[3,16,16,128]{3,2,1,0:T(8,128)(2,1)} %u_hbm.1), channel_id=1, source_target_pairs={{0,16},{1,17},{2,18},{3,19},{4,20},{5,21},{6,22},{7,23},{8,24},{9,... | collective-permute-start | bytes 589832 | tf_op jit(solution)/shard_map/ppermute | solution.py:42
  4.0 0.9 %copy-start = (bf16[3,16,16,128]{3,2,1,0:T(8,128)(2,1)S(1)}, bf16[3,16,16,128]{3,2,1,0:T(8,128)(2,1)}, u32[]{:S(2)}) copy-start(bf16[3,16,16,128]{3,2,1,0:T(8,128)(2,1)} %u_hbm.1) | copy-start | bytes 589828
  5.0 65.1 %copy-start.2 = (s32[5,16]{1,0:T(8,128)S(1)}, s32[5,16]{1,0:T(8,128)}, u32[]{:S(2)}) copy-start(s32[5,16]{1,0:T(8,128)} %index_ref.1) | copy-start | bytes 964
  5.0 65.1 %copy-start.3 = (f32[3,32]{1,0:T(4,128)S(1)}, f32[3,32]{1,0:T(4,128)}, u32[]{:S(2)}) copy-start(f32[3,32]{1,0:T(4,128)} %weight_ref.1) | copy-start | bytes 1156
  5.0 68.4 %copy-start.1 = (s32[5,3]{0,1:T(4,128)S(1)}, s32[5,3]{0,1:T(4,128)}, u32[]{:S(2)}) copy-start(s32[5,3]{0,1:T(4,128)} %param.5) | copy-start | bytes 184
  7.3 66.1 %collective-permute-start.6 = (bf16[2,3,16,16,128]{4,3,2,1,0:T(8,128)(2,1)S(1)}, bf16[2,3,16,16,128]{4,3,2,1,0:T(8,128)(2,1)S(1)}, u32[]{:S(2)}, u32[]{:S(2)}) collective-permute-start(bf16[2,3,16,16,128]{4,3,2,1,0:T(8,128)(2,1)S(1)} %shard_map.50), channel_id=1, source_target_pairs={{0,32},{1,33},{2,34},{3,35},{4,36},{5,37},{6,38},{7,39},{8,40},{9,... | collective-permute-start | bytes 1179656 | tf_op jit(solution)/shard_map/ppermute | solution.py:42
  13.6 20.1 %collective-permute-start = (bf16[3,16,16,128]{3,2,1,0:T(8,128)(2,1)S(1)}, bf16[3,16,16,128]{3,2,1,0:T(8,128)(2,1)S(1)}, u32[]{:S(2)}, u32[]{:S(2)}) collective-permute-start(bf16[3,16,16,128]{3,2,1,0:T(8,128)(2,1)S(1)} %copy-done), channel_id=1, source_target_pairs={{0,64},{1,65},{2,66},{3,67},{4,68},{5,69},{6,70},{7,71},{8,72},{9,... | collective-permute-start | bytes 589832 | tf_op jit(solution)/shard_map/ppermute | solution.py:42
  16.7 20.3 %collective-permute-start.1 = (bf16[3,16,16,128]{3,2,1,0:T(8,128)(2,1)S(1)}, bf16[3,16,16,128]{3,2,1,0:T(8,128)(2,1)S(1)}, u32[]{:S(2)}, u32[]{:S(2)}) collective-permute-start(bf16[3,16,16,128]{3,2,1,0:T(8,128)(2,1)S(1)} %copy-done), channel_id=1, source_target_pairs={{0,448},{1,449},{2,450},{3,451},{4,452},{5,453},{6,454},{7,455},{8... | collective-permute-start | bytes 589832 | tf_op jit(solution)/shard_map/ppermute | solution.py:42
  37.1 36.3 %collective-permute-start.2 = (bf16[3,3,16,4,128]{4,3,2,1,0:T(4,128)(2,1)S(1)}, bf16[3,3,16,4,128]{4,3,2,1,0:T(4,128)(2,1)S(1)}, u32[]{:S(2)}, u32[]{:S(2)}) collective-permute-start(bf16[3,3,16,4,128]{4,3,2,1,0:T(4,128)(2,1)S(1)} %shard_map.48), channel_id=1, source_target_pairs={{0,1},{1,0},{2,3},{3,2},{4,5},{5,4},{6,7},{7,6},{8,9},{9,8},{10,11... | collective-permute-start | bytes 442376 | tf_op jit(solution)/shard_map/ppermute | solution.py:42
  52.6 20.7 %collective-permute-start.3 = (bf16[2,3,16,4,128]{4,3,2,1,0:T(4,128)(2,1)S(1)}, bf16[2,3,16,4,128]{4,3,2,1,0:T(4,128)(2,1)S(1)}, u32[]{:S(2)}, u32[]{:S(2)}) collective-permute-start(bf16[2,3,16,4,128]{4,3,2,1,0:T(4,128)(2,1)S(1)} %shard_map.49), channel_id=1, source_target_pairs={{0,15},{1,2},{2,1},{3,4},{4,3},{5,6},{6,5},{7,8},{8,7},{9,10},{10,... | collective-permute-start | bytes 294920 | tf_op jit(solution)/shard_map/ppermute | solution.py:42
  56.0 17.4 %collective-permute-start.4 = (bf16[1,3,16,4,128]{4,3,2,1,0:T(4,128)(2,1)S(1)}, bf16[1,3,16,4,128]{4,3,2,1,0:T(4,128)(2,1)S(1)}, u32[]{:S(2)}, u32[]{:S(2)}) collective-permute-start(bf16[1,3,16,4,128]{4,3,2,1,0:T(4,128)(2,1)S(1)} %get-tuple-element.16), channel_id=1, source_target_pairs={{0,463},{1,450},{2,449},{3,452},{4,451},{5,454},{6,453},{7,456},{8... | collective-permute-start | bytes 147464 | tf_op jit(solution)/shard_map/ppermute | solution.py:42
  78.2 14.6 %collective-permute-start.7 = (f32[16,16,128]{2,1,0:T(8,128)S(1)}, f32[16,16,128]{2,1,0:T(8,128)S(1)}, u32[]{:S(2)}, u32[]{:S(2)}) collective-permute-start(f32[16,16,128]{2,1,0:T(8,128)S(1)} %get-tuple-element.18), channel_id=1, source_target_pairs={{0,16},{1,17},{2,18},{3,19},{4,20},{5,21},{6,22},{7,23},{8,24},{9,... | collective-permute-start | bytes 393224 | tf_op jit(solution)/shard_map/ppermute | solution.py:42
  80.5 12.3 %collective-permute-start.8 = (f32[16,16,128]{2,1,0:T(8,128)S(1)}, f32[16,16,128]{2,1,0:T(8,128)S(1)}, u32[]{:S(2)}, u32[]{:S(2)}) collective-permute-start(f32[16,16,128]{2,1,0:T(8,128)S(1)} %get-tuple-element.19), channel_id=1, source_target_pairs={{0,32},{1,33},{2,34},{3,35},{4,36},{5,37},{6,38},{7,39},{8,40},{9,... | collective-permute-start | bytes 393224 | tf_op jit(solution)/shard_map/ppermute | solution.py:42
  84.0 8.9 %collective-permute-start.9 = (f32[16,16,128]{2,1,0:T(8,128)S(1)}, f32[16,16,128]{2,1,0:T(8,128)S(1)}, u32[]{:S(2)}, u32[]{:S(2)}) collective-permute-start(f32[16,16,128]{2,1,0:T(8,128)S(1)} %get-tuple-element.20), channel_id=1, source_target_pairs={{0,48},{1,49},{2,50},{3,51},{4,52},{5,53},{6,54},{7,55},{8,56},{9,... | collective-permute-start | bytes 393224 | tf_op jit(solution)/shard_map/ppermute | solution.py:42

commit v4 on v3

--- a/solution.py
+++ b/solution.py
@@ -21,8 +21,8 @@
     return ((h * 4 + x) * 4 + y) * 16 + g
 
 
-def pairs(to):
-    every = [(h, x, y, g) for h in range(2) for x in range(4) for y in range(4) for g in range(16)]
+def pairs(to, rows=range(16)):
+    every = [(h, x, y, g) for h in range(2) for x in range(4) for y in range(4) for g in rows]
     return [(number(*p), number(*to(*p))) for p in every]
 
 
@@ -35,7 +35,8 @@
 SWAP_Y = [pairs(lambda h, x, y, g, k=k: (h, x, y ^ k, g)) for k in (1, 2, 3)]
 SWAP_E = pairs(lambda h, x, y, g: (h, x, y, g ^ 1))
 SWAP_O = pairs(lambda h, x, y, g: (h, x, y, beside(g)))
-SWAP_AO = pairs(lambda h, x, y, g: (h ^ (x % 3 == 0), 3 - x, y, beside(g)))
+SWAP_AO = pairs(lambda h, x, y, g: (h ^ (x % 3 == 0), 3 - x, y, beside(g)), (0, 15))
+SWAP_AN = pairs(lambda h, x, y, g: (h, x, y, beside(g)), range(1, 15))
 
 
 def send(x, perm):
@@ -187,7 +188,8 @@
     pack(rows, (u_ref, b_ref), 1)
 
 
-def third(u_ref, b_ref, a_ref, rows):
+def third(u_ref, b_ref, a_ref, rows, beside_rows):
+    pack(beside_rows, (a_ref,), 1)
     pack(rows, (u_ref, b_ref, a_ref), 0)
 
 
@@ -205,13 +207,13 @@
 
 
 def others(
-    lag_ref, field_in, gains, e_ref, o_ref, ao_ref, r_ref, both_ref,
+    lag_ref, field_in, gains, e_ref, o_ref, ao_ref, an_ref, r_ref, both_ref,
     field, out1, out2, out3, base, sums, *work,
 ):
     del field_in
     put_halo(field, 0, e_ref.at[0], o_ref.at[0])
     put_halo(field, 1, e_ref.at[1], o_ref.at[1])
-    put_halo(field, 2, e_ref.at[2], ao_ref.at[0])
+    put_halo(field, 2, e_ref.at[2], ao_ref[0].astype(jnp.float32) + an_ref[0].astype(jnp.float32))
     for slot, ref in enumerate((r_ref, both_ref.at[0], both_ref.at[1])):
         base[slot] = ref[...]
     sums[...] = jnp.zeros_like(sums)
@@ -270,11 +272,13 @@
     both = jax.ShapeDtypeStruct((2, *BLOCK.shape), BLOCK.dtype)
     both = send(call(pair, (), (u, r), both, 1 << 20), SWAP_Y[1])
     o = send(call(second, (), (u, b), edges(2), 1 << 20), SWAP_O)
-    e = send(call(third, (), (u, b, a), edges(3), 1 << 20), SWAP_E)
+    rows, beside_rows = call(third, (), (u, b, a), (edges(3), edges(1)), 1 << 20)
+    an = send(beside_rows, SWAP_AN)
+    e = send(rows, SWAP_E)
     field, gains = call(widen, (filter_index, filter_weights), (u, b, a), (FIELD, GAINS), 1 << 21)
     lags = lag_table.T
     field, s1, s2, s3 = call(
-        others, (lags,), (field, gains, e, o, ao, r, both),
+        others, (lags,), (field, gains, e, o, ao, an, r, both),
         (FIELD, PART, PART, PART), 3 << 23,
         [pltpu.VMEM((3, 3, PLANES, ROWS, LANES), jnp.bfloat16),
          pltpu.VMEM((4, PLANES, ROWS, LANES), jnp.float32), *WORK], {1: 0},

time: 93.9 us -> 90.1 us (0.960)
  the two profiles are of different devices: /device:TPU:1 before, /device:TPU:6 now
where the time goes in v4:
time: 90.1 us; the launch traced here: 89.7 us
  starting transfers between devices  58.1 us (64%)
  waiting for transfers between devices  18.6 us (21%)
  Pallas kernels  11.2 us (12%)
  local copies, waits for them, and re-layouts  0.94 us (1%)
    ppermute x11, starting transfers between devices, send(): return lax.ppermute(x, AXES, perm)  58.1 us
    ppermute x11, waiting for transfers between devices, send(): return lax.ppermute(x, AXES, perm)  18.6 us
    pallas_call x7, Pallas kernels, call(): pl.pallas_call(kernel, out_shape=outs, in_specs=[smem] * len(scalars) + [...  11.2 us
  transfers between devices with their start and end apart: 11, of which 3 were waited for; matrix products, arithmetic and copies ran while one was open for 0% of the time, Pallas kernels for 7%

profile of v4, /device:TPU:6, one launch (start us, length us, event | category | flops | bytes accessed | tf_op | source)
XLA Modules:
  0.0 89.7 jit_solution(17579531802420311340)
XLA Ops:
  0.0 3.5 %collective-permute-start.6 = (bf16[3,16,16,128]{3,2,1,0:T(8,128)(2,1)}, bf16[3,16,16,128]{3,2,1,0:T(8,128)(2,1)S(1)}, u32[]{:S(2)}, u32[]{:S(2)}) collective-permute-start(bf16[3,16,16,128]{3,2,1,0:T(8,128)(2,1)} %u_hbm.1), channel_id=1, source_target_pairs={{0,16},{1,17},{2,18},{3,19},{4,20},{5,21},{6,22},{7,23},{8,24},{9,... | collective-permute-start | bytes 589832 | tf_op jit(solution)/shard_map/ppermute | solution.py:43
  3.5 0.0 copy-start
  3.5 0.9 %copy-done = bf16[3,16,16,128]{3,2,1,0:T(8,128)(2,1)S(1)} copy-done((bf16[3,16,16,128]{3,2,1,0:T(8,128)(2,1)S(1)}, bf16[3,16,16,128]{3,2,1,0:T(8,128)(2,1)}, u32[]{:S(2)}) %copy-start) | copy-done | bytes 196632
  4.4 0.0 copy-start.2
  4.4 0.0 copy-start.3
  4.4 0.0 copy-start.1
  4.4 0.3 shard_map.46
  4.7 4.0 %collective-permute-done.6.r_ref = bf16[3,16,16,128]{3,2,1,0:T(8,128)(2,1)S(1)} collective-permute-done((bf16[3,16,16,128]{3,2,1,0:T(8,128)(2,1)}, bf16[3,16,16,128]{3,2,1,0:T(8,128)(2,1)S(1)}, u32[]{:S(2)}, u32[]{:S(2)}) %collective-permute-start.6) | collective-permute-done | bytes 196640 | tf_op jit(solution)/shard_map/ppermute | solution.py:43
  8.8 5.1 %collective-permute-start.7 = (bf16[2,3,16,16,128]{4,3,2,1,0:T(8,128)(2,1)S(1)}, bf16[2,3,16,16,128]{4,3,2,1,0:T(8,128)(2,1)S(1)}, u32[]{:S(2)}, u32[]{:S(2)}) collective-permute-start(bf16[2,3,16,16,128]{4,3,2,1,0:T(8,128)(2,1)S(1)} %shard_map.50), channel_id=1, source_target_pairs={{0,32},{1,33},{2,34},{3,35},{4,36},{5,37},{6,38},{7,39},{8,40},{9,... | collective-permute-start | bytes 1179656 | tf_op jit(solution)/shard_map/ppermute | solution.py:43
  13.9 2.7 %collective-permute-start = (bf16[3,16,16,128]{3,2,1,0:T(8,128)(2,1)S(1)}, bf16[3,16,16,128]{3,2,1,0:T(8,128)(2,1)S(1)}, u32[]{:S(2)}, u32[]{:S(2)}) collective-permute-start(bf16[3,16,16,128]{3,2,1,0:T(8,128)(2,1)S(1)} %copy-done), channel_id=1, source_target_pairs={{0,64},{1,65},{2,66},{3,67},{4,68},{5,69},{6,70},{7,71},{8,72},{9,... | collective-permute-start | bytes 589832 | tf_op jit(solution)/shard_map/ppermute | solution.py:43
  16.6 16.3 %collective-permute-start.1 = (bf16[3,16,16,128]{3,2,1,0:T(8,128)(2,1)S(1)}, bf16[3,16,16,128]{3,2,1,0:T(8,128)(2,1)S(1)}, u32[]{:S(2)}, u32[]{:S(2)}) collective-permute-start(bf16[3,16,16,128]{3,2,1,0:T(8,128)(2,1)S(1)} %copy-done), channel_id=1, source_target_pairs={{0,448},{1,449},{2,450},{3,451},{4,452},{5,453},{6,454},{7,455},{8... | collective-permute-start | bytes 589832 | tf_op jit(solution)/shard_map/ppermute | solution.py:43
  32.9 0.0 collective-permute-done.b_ref
  32.9 14.5 %collective-permute-done.1.a_ref = bf16[3,16,16,128]{3,2,1,0:T(8,128)(2,1)S(1)} collective-permute-done((bf16[3,16,16,128]{3,2,1,0:T(8,128)(2,1)S(1)}, bf16[3,16,16,128]{3,2,1,0:T(8,128)(2,1)S(1)}, u32[]{:S(2)}, u32[]{:S(2)}) %collective-permute-start.1) | collective-permute-done | bytes 196640 | tf_op jit(solution)/shard_map/ppermute | solution.py:43
  47.4 0.1 shard_map.48
  47.5 1.9 %collective-permute-start.2 = (bf16[3,3,16,4,128]{4,3,2,1,0:T(4,128)(2,1)S(1)}, bf16[3,3,16,4,128]{4,3,2,1,0:T(4,128)(2,1)S(1)}, u32[]{:S(2)}, u32[]{:S(2)}) collective-permute-start(bf16[3,3,16,4,128]{4,3,2,1,0:T(4,128)(2,1)S(1)} %get-tuple-element.18), channel_id=1, source_target_pairs={{0,1},{1,0},{2,3},{3,2},{4,5},{5,4},{6,7},{7,6},{8,9},{9,8},{10,11... | collective-permute-start | bytes 442376 | tf_op jit(solution)/shard_map/ppermute | solution.py:43
  49.5 7.6 %collective-permute-start.3 = (bf16[2,3,16,4,128]{4,3,2,1,0:T(4,128)(2,1)S(1)}, bf16[2,3,16,4,128]{4,3,2,1,0:T(4,128)(2,1)S(1)}, u32[]{:S(2)}, u32[]{:S(2)}) collective-permute-start(bf16[2,3,16,4,128]{4,3,2,1,0:T(4,128)(2,1)S(1)} %shard_map.49), channel_id=1, source_target_pairs={{0,15},{1,2},{2,1},{3,4},{4,3},{5,6},{6,5},{7,8},{8,7},{9,10},{10,... | collective-permute-start | bytes 294920 | tf_op jit(solution)/shard_map/ppermute | solution.py:43
  57.1 9.8 %collective-permute-start.4 = (bf16[1,3,16,4,128]{4,3,2,1,0:T(4,128)(2,1)S(1)}, bf16[1,3,16,4,128]{4,3,2,1,0:T(4,128)(2,1)S(1)}, u32[]{:S(2)}, u32[]{:S(2)}) collective-permute-start(bf16[1,3,16,4,128]{4,3,2,1,0:T(4,128)(2,1)S(1)} %get-tuple-element.19), channel_id=1, source_target_pairs={{0,463},{15,448},{16,479},{31,464},{32,495},{47,480},{48,511},{63,... | collective-permute-start | bytes 147464 | tf_op jit(solution)/shard_map/ppermute | solution.py:43
  66.9 0.7 collective-permute-start.5
  67.6 0.0 copy-done.2
  67.6 0.0 copy-done.3
  67.6 1.0 %shard_map.47 = (f32[3,3,16,24,128]{4,3,2,1,0:T(8,128)S(1)}, f32[80,3,8,128]{3,2,1,0:T(8,128)S(1)}) custom-call(s32[5,16]{1,0:T(8,128)S(1)} %copy-done.2, f32[3,32]{1,0:T(4,128)S(1)} %copy-done.3, bf16[3,16,16,128]{3,2,1,0:T(8,128)(2,1)S(1)} %get-tuple-element.15.u_ref, bf16[3,16,16,128]{3,2,1,0:T(8,128)(2,1)S(1)} %collective-permute-done.b_ref, ...), custom_call_target="tpu_custom_call" | custom-call | flops 2097152 | bytes 4194304 | tf_op jit(solution)/shard_map/pallas_call | solution.py:251
  68.6 0.1 collective-permute-done.4.ao_ref
  68.7 0.0 collective-permute-done.5.an_ref
  68.7 0.0 collective-permute-done.3.o_ref
  68.7 0.0 collective-permute-done.2.e_ref
  68.7 0.0 collective-permute-done.7.both_ref
  68.7 0.0 copy-done.1
  68.7 4.8 %shard_map.51 = (f32[3,3,16,24,128]{4,3,2,1,0:T(8,128)S(1)}, f32[16,16,128]{2,1,0:T(8,128)S(1)}, f32[16,16,128]{2,1,0:T(8,128)S(1)}, f32[16,16,128]{2,1,0:T(8,128)S(1)}) custom-call(s32[3,5]{1,0:T(4,128)S(1)} %bitcast.3, f32[3,3,16,24,128]{4,3,2,1,0:T(8,128)S(1)} %get-tuple-element.16.field_in, ...), custom_call_target="tpu_custom_call", output_to_operand_aliasing={{0}: (1, {})} | custom-call | flops 25165824 | bytes 4194304 | tf_op jit(solution)/shard_map/pallas_call | solution.py:251
  73.5 2.6 %collective-permute-start.8 = (f32[16,16,128]{2,1,0:T(8,128)S(1)}, f32[16,16,128]{2,1,0:T(8,128)S(1)}, u32[]{:S(2)}, u32[]{:S(2)}) collective-permute-start(f32[16,16,128]{2,1,0:T(8,128)S(1)} %get-tuple-element.22), channel_id=1, source_target_pairs={{0,16},{1,17},{2,18},{3,19},{4,20},{5,21},{6,22},{7,23},{8,24},{9,... | collective-permute-start | bytes 393224 | tf_op jit(solution)/shard_map/ppermute | solution.py:43
  76.1 3.7 %collective-permute-start.9 = (f32[16,16,128]{2,1,0:T(8,128)S(1)}, f32[16,16,128]{2,1,0:T(8,128)S(1)}, u32[]{:S(2)}, u32[]{:S(2)}) collective-permute-start(f32[16,16,128]{2,1,0:T(8,128)S(1)} %get-tuple-element.23), channel_id=1, source_target_pairs={{0,32},{1,33},{2,34},{3,35},{4,36},{5,37},{6,38},{7,39},{8,40},{9,... | collective-permute-start | bytes 393224 | tf_op jit(solution)/shard_map/ppermute | solution.py:43
  79.9 4.1 %collective-permute-start.10 = (f32[16,16,128]{2,1,0:T(8,128)S(1)}, f32[16,16,128]{2,1,0:T(8,128)S(1)}, u32[]{:S(2)}, u32[]{:S(2)}) collective-permute-start(f32[16,16,128]{2,1,0:T(8,128)S(1)} %get-tuple-element.24), channel_id=1, source_target_pairs={{0,48},{1,49},{2,50},{3,51},{4,52},{5,53},{6,54},{7,55},{8,56},{9,... | collective-permute-start | bytes 393224 | tf_op jit(solution)/shard_map/ppermute | solution.py:43
  84.0 5.0 %shard_map.52 = f32[16,16,128]{2,1,0:T(8,128)S(1)} custom-call(s32[3,5]{1,0:T(4,128)S(1)} %bitcast.4, f32[3,3,16,24,128]{4,3,2,1,0:T(8,128)S(1)} %get-tuple-element.21.field, f32[80,3,8,128]{3,2,1,0:T(8,128)S(1)} %get-tuple-element.17.gains, bf16[1,3,16,16,128]{4,3,2,1,0:T(8,128)(2,1)S(1)} %bitcast.2), custom_call_target="tpu_custom_call" | custom-call | flops 25165824 | bytes 4194304 | tf_op jit(solution)/shard_map/pallas_call | solution.py:251
  89.0 0.0 collective-permute-done.8
  89.0 0.0 collective-permute-done.9
  89.0 0.0 collective-permute-done.10
  89.1 0.7 add_multiply_fusion
  (2 shorter events, 0.1 us)
Async XLA Ops:
  0.0 8.7 %collective-permute-start.6 = (bf16[3,16,16,128]{3,2,1,0:T(8,128)(2,1)}, bf16[3,16,16,128]{3,2,1,0:T(8,128)(2,1)S(1)}, u32[]{:S(2)}, u32[]{:S(2)}) collective-permute-start(bf16[3,16,16,128]{3,2,1,0:T(8,128)(2,1)} %u_hbm.1), channel_id=1, source_target_pairs={{0,16},{1,17},{2,18},{3,19},{4,20},{5,21},{6,22},{7,23},{8,24},{9,... | collective-permute-start | bytes 589832 | tf_op jit(solution)/shard_map/ppermute | solution.py:43
  3.5 0.9 %copy-start = (bf16[3,16,16,128]{3,2,1,0:T(8,128)(2,1)S(1)}, bf16[3,16,16,128]{3,2,1,0:T(8,128)(2,1)}, u32[]{:S(2)}) copy-start(bf16[3,16,16,128]{3,2,1,0:T(8,128)(2,1)} %u_hbm.1) | copy-start | bytes 589828
  4.4 63.2 %copy-start.2 = (s32[5,16]{1,0:T(8,128)S(1)}, s32[5,16]{1,0:T(8,128)}, u32[]{:S(2)}) copy-start(s32[5,16]{1,0:T(8,128)} %index_ref.1) | copy-start | bytes 964
  4.4 63.2 %copy-start.3 = (f32[3,32]{1,0:T(4,128)S(1)}, f32[3,32]{1,0:T(4,128)}, u32[]{:S(2)}) copy-start(f32[3,32]{1,0:T(4,128)} %weight_ref.1) | copy-start | bytes 1156
  4.4 64.3 %copy-start.1 = (s32[5,3]{0,1:T(4,128)S(1)}, s32[5,3]{0,1:T(4,128)}, u32[]{:S(2)}) copy-start(s32[5,3]{0,1:T(4,128)} %param.5) | copy-start | bytes 184
  8.8 59.9 %collective-permute-start.7 = (bf16[2,3,16,16,128]{4,3,2,1,0:T(8,128)(2,1)S(1)}, bf16[2,3,16,16,128]{4,3,2,1,0:T(8,128)(2,1)S(1)}, u32[]{:S(2)}, u32[]{:S(2)}) collective-permute-start(bf16[2,3,16,16,128]{4,3,2,1,0:T(8,128)(2,1)S(1)} %shard_map.50), channel_id=1, source_target_pairs={{0,32},{1,33},{2,34},{3,35},{4,36},{5,37},{6,38},{7,39},{8,40},{9,... | collective-permute-start | bytes 1179656 | tf_op jit(solution)/shard_map/ppermute | solution.py:43
  13.9 19.1 %collective-permute-start = (bf16[3,16,16,128]{3,2,1,0:T(8,128)(2,1)S(1)}, bf16[3,16,16,128]{3,2,1,0:T(8,128)(2,1)S(1)}, u32[]{:S(2)}, u32[]{:S(2)}) collective-permute-start(bf16[3,16,16,128]{3,2,1,0:T(8,128)(2,1)S(1)} %copy-done), channel_id=1, source_target_pairs={{0,64},{1,65},{2,66},{3,67},{4,68},{5,69},{6,70},{7,71},{8,72},{9,... | collective-permute-start | bytes 589832 | tf_op jit(solution)/shard_map/ppermute | solution.py:43
  16.6 30.8 %collective-permute-start.1 = (bf16[3,16,16,128]{3,2,1,0:T(8,128)(2,1)S(1)}, bf16[3,16,16,128]{3,2,1,0:T(8,128)(2,1)S(1)}, u32[]{:S(2)}, u32[]{:S(2)}) collective-permute-start(bf16[3,16,16,128]{3,2,1,0:T(8,128)(2,1)S(1)} %copy-done), channel_id=1, source_target_pairs={{0,448},{1,449},{2,450},{3,451},{4,452},{5,453},{6,454},{7,455},{8... | collective-permute-start | bytes 589832 | tf_op jit(solution)/shard_map/ppermute | solution.py:43
  47.5 21.2 %collective-permute-start.2 = (bf16[3,3,16,4,128]{4,3,2,1,0:T(4,128)(2,1)S(1)}, bf16[3,3,16,4,128]{4,3,2,1,0:T(4,128)(2,1)S(1)}, u32[]{:S(2)}, u32[]{:S(2)}) collective-permute-start(bf16[3,3,16,4,128]{4,3,2,1,0:T(4,128)(2,1)S(1)} %get-tuple-element.18), channel_id=1, source_target_pairs={{0,1},{1,0},{2,3},{3,2},{4,5},{5,4},{6,7},{7,6},{8,9},{9,8},{10,11... | collective-permute-start | bytes 442376 | tf_op jit(solution)/shard_map/ppermute | solution.py:43
  49.5 19.2 %collective-permute-start.3 = (bf16[2,3,16,4,128]{4,3,2,1,0:T(4,128)(2,1)S(1)}, bf16[2,3,16,4,128]{4,3,2,1,0:T(4,128)(2,1)S(1)}, u32[]{:S(2)}, u32[]{:S(2)}) collective-permute-start(bf16[2,3,16,4,128]{4,3,2,1,0:T(4,128)(2,1)S(1)} %shard_map.49), channel_id=1, source_target_pairs={{0,15},{1,2},{2,1},{3,4},{4,3},{5,6},{6,5},{7,8},{8,7},{9,10},{10,... | collective-permute-start | bytes 294920 | tf_op jit(solution)/shard_map/ppermute | solution.py:43
  57.1 11.6 %collective-permute-start.4 = (bf16[1,3,16,4,128]{4,3,2,1,0:T(4,128)(2,1)S(1)}, bf16[1,3,16,4,128]{4,3,2,1,0:T(4,128)(2,1)S(1)}, u32[]{:S(2)}, u32[]{:S(2)}) collective-permute-start(bf16[1,3,16,4,128]{4,3,2,1,0:T(4,128)(2,1)S(1)} %get-tuple-element.19), channel_id=1, source_target_pairs={{0,463},{15,448},{16,479},{31,464},{32,495},{47,480},{48,511},{63,... | collective-permute-start | bytes 147464 | tf_op jit(solution)/shard_map/ppermute | solution.py:43
  66.9 1.8 %collective-permute-start.5 = (bf16[1,3,16,4,128]{4,3,2,1,0:T(4,128)(2,1)S(1)}, bf16[1,3,16,4,128]{4,3,2,1,0:T(4,128)(2,1)S(1)}, u32[]{:S(2)}, u32[]{:S(2)}) collective-permute-start(bf16[1,3,16,4,128]{4,3,2,1,0:T(4,128)(2,1)S(1)} %get-tuple-element.20), channel_id=1, source_target_pairs={{1,2},{2,1},{3,4},{4,3},{5,6},{6,5},{7,8},{8,7},{9,10},{10,9},{11,... | collective-permute-start | bytes 147464 | tf_op jit(solution)/shard_map/ppermute | solution.py:43
  73.5 15.5 %collective-permute-start.8 = (f32[16,16,128]{2,1,0:T(8,128)S(1)}, f32[16,16,128]{2,1,0:T(8,128)S(1)}, u32[]{:S(2)}, u32[]{:S(2)}) collective-permute-start(f32[16,16,128]{2,1,0:T(8,128)S(1)} %get-tuple-element.22), channel_id=1, source_target_pairs={{0,16},{1,17},{2,18},{3,19},{4,20},{5,21},{6,22},{7,23},{8,24},{9,... | collective-permute-start | bytes 393224 | tf_op jit(solution)/shard_map/ppermute | solution.py:43
  76.1 12.9 %collective-permute-start.9 = (f32[16,16,128]{2,1,0:T(8,128)S(1)}, f32[16,16,128]{2,1,0:T(8,128)S(1)}, u32[]{:S(2)}, u32[]{:S(2)}) collective-permute-start(f32[16,16,128]{2,1,0:T(8,128)S(1)} %get-tuple-element.23), channel_id=1, source_target_pairs={{0,32},{1,33},{2,34},{3,35},{4,36},{5,37},{6,38},{7,39},{8,40},{9,... | collective-permute-start | bytes 393224 | tf_op jit(solution)/shard_map/ppermute | solution.py:43
  79.9 9.1 %collective-permute-start.10 = (f32[16,16,128]{2,1,0:T(8,128)S(1)}, f32[16,16,128]{2,1,0:T(8,128)S(1)}, u32[]{:S(2)}, u32[]{:S(2)}) collective-permute-start(f32[16,16,128]{2,1,0:T(8,128)S(1)} %get-tuple-element.24), channel_id=1, source_target_pairs={{0,48},{1,49},{2,50},{3,51},{4,52},{5,53},{6,54},{7,55},{8,56},{9,... | collective-permute-start | bytes 393224 | tf_op jit(solution)/shard_map/ppermute | solution.py:43
